TPU v7x, 32 devices: a whole 2x2x4 slice. The times are simulated.
32 devices in a mesh: groups: 2 (over y), tx: 16 (over z, x, core).
Axes of the slice: x: 2, y: 2, z: 4, core: 2. Of those that a mesh axis runs over, the one named last changes fastest.
Arguments:
- tile_state: bfloat16 [64, 64, 64, 128], P(('groups', 'tx')), parts along dimension 0, may hold values from -6 to 6
- cotangent: bfloat16 [64, 64, 64, 128], P(('groups', 'tx')), parts along dimension 0, may hold values from -6 to 6
- neighbours: int32 [64, 8], P(('groups', 'tx')), parts along dimension 0, may hold values from -1 to 31, as said below
- land_mask: int32 [64, 4096], P(('groups', 'tx')), parts along dimension 0, may hold values 0 or 1
- kernel: float32 [49, 128], replicated, may hold values from -0.875 to 0.875
- conv_bias: float32 [128], replicated, may hold values from -3 to 3
- norm_gain: float32 [128], replicated, may hold values from 0.25 to 1.75
- norm_bias: float32 [128], replicated, may hold values from -3 to 3
- w_up: bfloat16 [512, 128], replicated, may hold values from -0.5 to 0.5
- up_bias: float32 [512], replicated, may hold values from -3 to 3
- w_down: bfloat16 [512, 128], replicated, may hold values from -0.25 to 0.25
- down_bias: float32 [128], replicated, may hold values from -3 to 3
- layer_scale: float32 [128], replicated, may hold values from 0.3 to 1
Outputs:
- block_out: bfloat16 [64, 64, 64, 128], P(('groups', 'tx')), parts along dimension 0
- grad_state: bfloat16 [64, 64, 64, 128], P(('groups', 'tx')), parts along dimension 0
- grad_up: float32 [1024, 128], P(('groups', 'tx')), parts along dimension 0
- grad_down: float32 [1024, 128], P(('groups', 'tx')), parts along dimension 0
- grad_kernel: float32 [98, 128], P('groups'), parts along dimension 0
- grad_vectors: float32 [10, 128], P('groups'), parts along dimension 0
- grad_up_bias: float32 [1024], P('groups'), parts along dimension 0
There are 2 independent parts, one for each index of `groups`. A program takes and returns all parts, laid end to end along the dimension named above; an argument that names none is the same for every part. Nothing has to cross between parts.
Inputs may be any that keep to these rules, and one draw needn't show every extreme that they name: `neighbours`: each entry is -1 or the slot of another tile whose slot // 2 differs from the tile's own slot // 2 by at most 2, and that distance is reached. Neighbour relations are mutual: if u is t's neighbour in one direction, t is u's neighbour in the opposite direction.
All inputs are finite; a program needn't handle non-finite values. No bound on the sum of `land_mask` on one device may be relied on, other than what follows from the above.
Results may differ from a plain program's by a relative error of at most 0.0063.
Values may be sent and summed in bfloat16 or wider, within the bound.
No kernel may reach another device: no remote copies, remote signals or barrier semaphores. Data moves between devices by JAX's collectives and lax.ppermute only.
A program may use at most 128 MiB of HBM per device.

v0:
```python
import functools

import jax
import jax.numpy as jnp
from jax import lax
from jax.experimental import pallas as pl
from jax.experimental.pallas import tpu as pltpu
from jax.sharding import PartitionSpec as P

REACH = 2
HALO = 3
KSIZE = 7
TAPS = KSIZE * KSIZE
ROWS = 8
CONV_ROWS = 16
FCHUNK = 256
CELLS = 256
STEP_ROWS = 16
VMEM_MIB = 58

EPSILON = 1e-06
INV_SQRT2 = 0.7071067811865476
INV_SQRT2PI = 0.3989422804014327
LOG2E = 1.4426950408889634

F32 = jnp.float32
BF16 = jnp.bfloat16
NT = (((1,), (1,)), ((), ()))


def shifted(shard, axis, by):
    count = lax.axis_size(axis)
    pairs = [(i, i + by) for i in range(count) if 0 <= i + by < count]
    return lax.ppermute(shard, axis, pairs)


def params(limit_mib, side=False):
    return pltpu.CompilerParams(vmem_limit_bytes=limit_mib << 20)


def spread(rows, chans):
    height = rows.shape[0]
    row = lax.broadcasted_iota(jnp.int32, (height, height * chans), 0)
    lane = lax.broadcasted_iota(jnp.int32, (height, height * chans), 1)
    pick = ((lane >= row * chans) & (lane < (row + 1) * chans)).astype(F32).astype(BF16)
    wide = jnp.dot(rows.T.astype(BF16), pick, preferred_element_type=F32)
    return [wide[:, r * chans : (r + 1) * chans] for r in range(height)]


def bands_kernel(state_ref, mask_ref, out_ref, left, right):
    edge = state_ref.shape[1]
    low = edge - HALO
    upper = mask_ref[0, 0:8].T
    lower = mask_ref[0, edge - 8 :].T
    for q in range(HALO):
        out_ref[0, 0, q] = (state_ref[0, q].astype(F32) * upper[:, q : q + 1]).astype(BF16)
        p = 8 - HALO + q
        out_ref[0, 1, q] = (state_ref[0, low + q].astype(F32) * lower[:, p : p + 1]).astype(BF16)
    left[...] = state_ref[0, :, 0:16].astype(F32).reshape(left.shape)
    right[...] = state_ref[0, :, edge - 16 :].astype(F32).reshape(right.shape)
    for q in range(HALO):
        out_ref[0, 2, q] = (
            left[pl.ds(q, edge, stride=16), :] * mask_ref[0, :, q : q + 1]
        ).astype(BF16)
        out_ref[0, 3, q] = (
            right[pl.ds(16 - HALO + q, edge, stride=16), :] * mask_ref[0, :, low + q : low + q + 1]
        ).astype(BF16)


def bands_call(state, mask):
    slots, edge, _, chans = state.shape
    return pl.pallas_call(
        bands_kernel,
        grid=(slots,),
        in_specs=[
            pl.BlockSpec((1, edge, edge, chans), lambda s: (s, 0, 0, 0)),
            pl.BlockSpec((1, edge, edge), lambda s: (s, 0, 0)),
        ],
        out_specs=pl.BlockSpec((1, 4, HALO, edge, chans), lambda s: (s, 0, 0, 0, 0)),
        out_shape=jax.ShapeDtypeStruct((slots, 4, HALO, edge, chans), BF16),
        scratch_shapes=[pltpu.VMEM((edge * 16, chans), F32)] * 2,
        compiler_params=params(VMEM_MIB),
        name="bands",
    )(state, mask)


def tap(weight_ref, index, chans):
    return jnp.broadcast_to(weight_ref[index : index + 1, :], (8, chans))


def conv_rows(padded, weight_ref, row, column, write, chans):
    totals = [None] * CONV_ROWS
    for b in range(KSIZE):
        weights = [tap(weight_ref, a * KSIZE + b, chans) for a in range(KSIZE)]
        for r in range(CONV_ROWS + KSIZE - 1):
            cells = padded[row + r, pl.ds(column + b, 8), :]
            for a in range(KSIZE):
                i = r - a
                if 0 <= i < CONV_ROWS:
                    term = cells * weights[a]
                    totals[i] = term if totals[i] is None else totals[i] + term
    for i in range(CONV_ROWS):
        write(i, totals[i])


def zero_margins(padded):
    rows, cols, chans = padded.shape
    padded[0:HALO] = jnp.zeros((HALO, cols, chans), F32)
    padded[rows - HALO :] = jnp.zeros((HALO, cols, chans), F32)

    def body(r, carry):
        padded[r, 0:8] = jnp.zeros((8, chans), F32)
        padded[r, cols - 8 :] = jnp.zeros((8, chans), F32)
        return carry

    lax.fori_loop(HALO, rows - HALO, body, 0)


def fill_masked(padded, state_ref, mask_ref):
    edge, chans = state_ref.shape[1], state_ref.shape[3]

    def body(n, carry):
        slabs = spread(mask_ref[0, pl.ds(pl.multiple_of(n * 8, 8), 8)], chans)
        for r in range(8):
            i = n * 8 + r
            padded[HALO + i, HALO : HALO + edge] = state_ref[0, i].astype(F32) * slabs[r]
        return carry

    lax.fori_loop(0, edge // 8, body, 0, unroll=4)


def conv_tile(padded, weight_ref, out_ref):
    edge, chans = out_ref.shape[1], out_ref.shape[3]

    def body(n, carry):
        for g in range(edge // 8):

            def write(i, value):
                out_ref[0, n * CONV_ROWS + i, g * 8 : g * 8 + 8] = value

            conv_rows(padded, weight_ref, n * CONV_ROWS, g * 8, write, chans)
        return carry

    lax.fori_loop(0, edge // CONV_ROWS, body, 0)


def own_conv_kernel(state_ref, mask_ref, weight_ref, out_ref, padded):
    zero_margins(padded)
    fill_masked(padded, state_ref, mask_ref)
    conv_tile(padded, weight_ref, out_ref)


def padded_shape(edge, chans):
    return (edge + 2 * HALO, edge + 8, chans)


def conv_cost(slots, edge, chans):
    cells = slots * edge * edge * chans
    return pl.CostEstimate(flops=2 * TAPS * cells, bytes_accessed=8 * cells, transcendentals=0)


def own_conv_call(state, mask, weights):
    slots, edge, _, chans = state.shape
    return pl.pallas_call(
        own_conv_kernel,
        grid=(slots,),
        in_specs=[
            pl.BlockSpec((1, edge, edge, chans), lambda s: (s, 0, 0, 0)),
            pl.BlockSpec((1, edge, edge), lambda s: (s, 0, 0)),
            pl.BlockSpec((TAPS, chans), lambda s: (0, 0)),
        ],
        out_specs=pl.BlockSpec((1, edge, edge, chans), lambda s: (s, 0, 0, 0)),
        out_shape=jax.ShapeDtypeStruct((slots, edge, edge, chans), F32),
        scratch_shapes=[pltpu.VMEM(padded_shape(edge, chans), F32)],
        compiler_params=params(VMEM_MIB),
        cost_estimate=conv_cost(slots, edge, chans),
        name="own_conv",
    )(state, mask, weights)


def load_window(sources, window, sem):
    slots = sources[0].shape[0]
    copies = [
        pltpu.make_async_copy(source, window.at[pl.ds(k * slots, slots)], sem.at[k])
        for k, source in enumerate(sources)
    ]
    for copy in copies:
        copy.start()
    for copy in copies:
        copy.wait()


def picked(window, slot_ref, here_ref, tile, direction, which, q):
    band = window[slot_ref[tile, direction], which, q].astype(F32)
    return jnp.where(here_ref[tile, direction] > 0, band, jnp.zeros_like(band))


def fill_rows(north, south, window, slot_ref, here_ref, tile):
    edge = window.shape[3]
    low = edge - HALO
    for q in range(HALO):
        for target, edge_dir, which, left_dir, right_dir in (
            (north, 0, 1, 4, 5),
            (south, 1, 0, 6, 7),
        ):
            target[q, HALO : HALO + edge] = picked(
                window, slot_ref, here_ref, tile, edge_dir, which, q
            )
            target[q, 0:HALO] = picked(window, slot_ref, here_ref, tile, left_dir, which, q)[low:]
            target[q, HALO + edge : HALO + edge + HALO] = picked(
                window, slot_ref, here_ref, tile, right_dir, which, q
            )[0:HALO]


def fill_columns(west, east, window, slot_ref, here_ref, tile):
    edge = window.shape[3]
    for q in range(HALO):
        west[pl.ds(HALO * 16 + q, edge, stride=16), :] = picked(
            window, slot_ref, here_ref, tile, 2, 3, q
        )
        east[pl.ds(HALO * 16 + 8 + HALO + q, edge, stride=16), :] = picked(
            window, slot_ref, here_ref, tile, 3, 2, q
        )


def fill_margins(padded, window, slot_ref, here_ref, tile):
    rows, stride, chans = padded.shape
    edge = window.shape[3]
    fill_rows(padded.at[0:HALO], padded.at[HALO + edge :], window, slot_ref, here_ref, tile)
    flat = padded.reshape(rows * stride, chans)
    for q in range(HALO):
        flat[pl.ds(HALO * stride + q, edge, stride=stride), :] = picked(
            window, slot_ref, here_ref, tile, 2, 3, q
        )
        flat[pl.ds(HALO * stride + HALO + edge + q, edge, stride=stride), :] = picked(
            window, slot_ref, here_ref, tile, 3, 2, q
        )


def clear_margins(north, south, west, east):
    for ref in (north, south, west, east):
        ref[...] = jnp.zeros_like(ref)


def add_columns(west, east, weight_ref, row, target, base, chans):
    edge = target.shape[1]
    for source, first, taps in ((west, 0, range(HALO)), (east, edge - 8, range(HALO + 1, KSIZE))):
        totals = [target[base + i, first : first + 8] for i in range(ROWS)]
        for b in taps:
            weights = [tap(weight_ref, a * KSIZE + b, chans) for a in range(KSIZE)]
            for r in range(ROWS + KSIZE - 1):
                cells = source[pl.ds((row + r) * 16 + b, 8), :]
                for a in range(KSIZE):
                    i = r - a
                    if 0 <= i < ROWS:
                        totals[i] = totals[i] + cells * weights[a]
        for i in range(ROWS):
            target[base + i, first : first + 8] = totals[i]


def add_rows(source, weight_ref, target, upper, chans):
    height, edge = target.shape[0], target.shape[1]
    pairs = []
    for q in range(HALO):
        for a in range(KSIZE):
            i = q - a if upper else HALO + q + height - a
            if 0 <= i < height:
                pairs.append((q, a, i))
    for g in range(edge // 8):
        rows = sorted({i for _, _, i in pairs})
        totals = {i: target[i, g * 8 : g * 8 + 8] for i in rows}
        for b in range(KSIZE):
            for q in range(HALO):
                cells = source[q, pl.ds(g * 8 + b, 8), :]
                for p, a, i in pairs:
                    if p == q:
                        totals[i] = totals[i] + cells * tap(weight_ref, a * KSIZE + b, chans)
        for i in rows:
            target[i, g * 8 : g * 8 + 8] = totals[i]


def window_scratch(slots, edge, chans):
    return [
        pltpu.VMEM(((2 * REACH + 1) * slots, 4, HALO, edge, chans), BF16),
        pltpu.SemaphoreType.DMA((2 * REACH + 1,)),
    ]


def margin_scratch(slots, edge, chans):
    return window_scratch(slots, edge, chans) + [
        pltpu.VMEM((HALO, edge + 8, chans), F32),
        pltpu.VMEM((HALO, edge + 8, chans), F32),
        pltpu.VMEM(((edge + 2 * HALO) * 16, chans), F32),
        pltpu.VMEM(((edge + 2 * HALO) * 16, chans), F32),
    ]


def margin_setup(sources, slot_ref, here_ref, scratch):
    window, sem, north, south, west, east = scratch
    tile, block = pl.program_id(0), pl.program_id(1)

    @pl.when((tile == 0) & (block == 0))
    def _():
        load_window(sources, window, sem)
        clear_margins(north, south, west, east)

    @pl.when(block == 0)
    def _():
        fill_rows(north, south, window, slot_ref, here_ref, tile)
        fill_columns(west, east, window, slot_ref, here_ref, tile)


def margin_add(weight_ref, target, scratch, chans):
    _, _, north, south, west, east = scratch
    block, blocks = pl.program_id(1), pl.num_programs(1)
    height = target.shape[0]

    def body(n, carry):
        add_columns(west, east, weight_ref, block * height + n * ROWS, target, n * ROWS, chans)
        return carry

    lax.fori_loop(0, height // ROWS, body, 0)

    @pl.when(block == 0)
    def _():
        add_rows(north, weight_ref, target, True, chans)

    @pl.when(block == blocks - 1)
    def _():
        add_rows(south, weight_ref, target, False, chans)


def folded(values):
    cells, chans = values.shape
    return jnp.sum(values.reshape(cells // 8, 8, chans), 0)


def mlp_cells(parts, par, acc):
    bias, gain, nbias, wup, upb, wdown, dbias, scale, wup_t, wdown_t = par
    gup, gdown, upacc, vec = acc
    units = wup.shape[0]
    chans = wup.shape[1]
    upper = []
    for conv, cot, mask in parts:
        conv = conv + bias[...]
        centred = conv - jnp.mean(conv, axis=-1, keepdims=True)
        inv_std = lax.rsqrt(jnp.mean(centred * centred, axis=-1, keepdims=True) + EPSILON)
        normal = centred * inv_std
        hidden = (normal * gain[...] + nbias[...]).astype(BF16)
        cotm = cot * mask
        dbranch = cotm * scale[...]
        upper.append((normal, inv_std, hidden, cotm, dbranch, dbranch.astype(BF16)))
    acts, dpres = [], []
    for f in range(0, units, FCHUNK):
        part = slice(f, f + FCHUNK)
        total = upacc[part]
        for _, _, hidden, _, _, dbranch_b in upper:
            cells = hidden.shape[0]
            pre = lax.dot_general(wup[part], hidden, NT, preferred_element_type=F32)
            pre = pre + jnp.concatenate([upb[part]] * (cells // 128), 1)
            dact = lax.dot_general(wdown[part], dbranch_b, NT, preferred_element_type=F32)
            cumul = 0.5 + 0.5 * lax.erf(pre * INV_SQRT2)
            slope = cumul + pre * (jnp.exp(-0.5 * pre * pre) * INV_SQRT2PI)
            dpre = dact * slope
            acts.append((pre * cumul).astype(BF16))
            dpres.append(dpre.astype(BF16))
            for lane in range(0, cells, 128):
                total = total + dpre[:, lane : lane + 128]
        upacc[part] = total
    count = len(parts)
    results = []
    sums = [vec[k] for k in range(5)]
    ups, downs = [], []
    for h, (normal, inv_std, hidden, cotm, dbranch, dbranch_b) in enumerate(upper):
        act = jnp.concatenate(acts[h::count], 0)
        dpre_b = jnp.concatenate(dpres[h::count], 0)
        ups.append(jnp.dot(dpre_b, hidden, preferred_element_type=F32))
        downs.append(jnp.dot(act, dbranch_b, preferred_element_type=F32))
        branch = jnp.dot(wdown_t[...], act, preferred_element_type=F32).T + dbias[...]
        dhidden = jnp.dot(wup_t[...], dpre_b, preferred_element_type=F32).T
        dnormal = dhidden * gain[...]
        dconv = inv_std * (
            dnormal
            - jnp.mean(dnormal, axis=-1, keepdims=True)
            - normal * jnp.mean(dnormal * normal, axis=-1, keepdims=True)
        )
        for k, values in enumerate((dconv, dhidden * normal, dhidden, dbranch, cotm * branch)):
            sums[k] = sums[k] + folded(values)
        results.append((branch, dconv))
    gup[...] += sum(ups[1:], ups[0])
    gdown[...] += sum(downs[1:], downs[0])
    for k in range(5):
        vec[k] = sums[k]
    return results


def mlp_kernel(slot_ref, here_ref, *refs):
    sources = refs[:5]
    conv_ref, state_ref, cot_ref, mask_ref, weight_ref = refs[5:10]
    bias, gain, nbias, wup, upb, wdown, dbias, scale = refs[10:18]
    out_ref, grad_ref, bands_ref, gup, gdown, upacc, vec = refs[18:25]
    conv_s, tile_grad, wup_t, wdown_t, upb_s = refs[25:30]
    scratch = refs[30:]
    par = (bias, gain, nbias, wup, upb_s, wdown, dbias, scale, wup_t, wdown_t)
    tile, block, blocks = pl.program_id(0), pl.program_id(1), pl.num_programs(1)
    height, edge, chans = conv_s.shape
    low = edge - HALO

    @pl.when((tile == 0) & (block == 0))
    def _():
        for ref in (gup, gdown, upacc, vec):
            ref[...] = jnp.zeros_like(ref)
        wup_t[...] = wup[...].astype(F32).T.astype(BF16)
        wdown_t[...] = wdown[...].astype(F32).T.astype(BF16)
        upb_s[...] = jnp.broadcast_to(upb[...], (128, upb.shape[1])).T

    margin_setup(sources, slot_ref, here_ref, scratch)
    conv_s[...] = conv_ref[0]
    margin_add(weight_ref, conv_s, scratch, chans)
    rows = CELLS // edge

    def body(n, carry):
        slabs = spread(mask_ref[0, pl.ds(pl.multiple_of(n * ROWS, ROWS), ROWS)], chans)
        parts, places, masks = [], [], []
        for h in range(ROWS // rows):
            first = n * ROWS + h * rows
            place = pl.ds(first, rows)
            mask = jnp.concatenate(slabs[h * rows : (h + 1) * rows], 0)
            places.append((first, place))
            masks.append(mask)
            parts.append(
                (
                    conv_s[place].reshape(CELLS, chans),
                    cot_ref[0, place].astype(F32).reshape(CELLS, chans),
                    mask,
                )
            )
        results = mlp_cells(parts, par, (gup, gdown, upacc, vec))
        for (first, place), mask, (branch, dconv) in zip(places, masks, results):
            state = state_ref[0, place].astype(F32).reshape(CELLS, chans)
            output = (state + (mask * scale[...]) * branch).astype(BF16)
            out_ref[0, place] = output.reshape(rows, edge, chans)
            grad_ref[0, place] = dconv.reshape(rows, edge, chans)
            start = pl.multiple_of((block * height + first) * edge, CELLS)
            tile_grad[pl.ds(start, CELLS), :] = dconv
        return carry

    lax.fori_loop(0, height // ROWS, body, 0)

    @pl.when(block == blocks - 1)
    def _():
        for q in range(HALO):
            bands_ref[0, 0, q] = tile_grad[q * edge : (q + 1) * edge].astype(BF16)
            bands_ref[0, 1, q] = tile_grad[(low + q) * edge : (low + q + 1) * edge].astype(BF16)
            bands_ref[0, 2, q] = tile_grad[pl.ds(q, edge, stride=edge), :].astype(BF16)
            bands_ref[0, 3, q] = tile_grad[pl.ds(low + q, edge, stride=edge), :].astype(BF16)


def mlp_call(slot, here, sources, conv, state, cot, mask, weights, par):
    slots, edge, _, chans = state.shape
    units = par[3].shape[0]
    blocks = edge // STEP_ROWS
    row_spec = pl.BlockSpec((1, STEP_ROWS, edge, chans), lambda s, n, *_: (s, n, 0, 0))

    def whole(a):
        return pl.BlockSpec(a.shape, lambda s, n, *_: (0,) * a.ndim)

    grid_spec = pltpu.PrefetchScalarGridSpec(
        num_scalar_prefetch=2,
        grid=(slots, blocks),
        in_specs=[pl.BlockSpec(memory_space=pl.ANY)] * 5
        + [
            row_spec,
            row_spec,
            row_spec,
            pl.BlockSpec((1, STEP_ROWS, edge), lambda s, n, *_: (s, n, 0)),
            whole(weights),
        ]
        + [whole(a) for a in par],
        out_specs=[
            row_spec,
            row_spec,
            pl.BlockSpec((1, 4, HALO, edge, chans), lambda s, n, *_: (s, 0, 0, 0, 0)),
            pl.BlockSpec((units, chans), lambda s, n, *_: (0, 0)),
            pl.BlockSpec((units, chans), lambda s, n, *_: (0, 0)),
            pl.BlockSpec((units, 128), lambda s, n, *_: (0, 0)),
            pl.BlockSpec((5, 8, chans), lambda s, n, *_: (0, 0, 0)),
        ],
        scratch_shapes=[
            pltpu.VMEM((STEP_ROWS, edge, chans), F32),
            pltpu.VMEM((edge * edge, chans), F32),
            pltpu.VMEM((chans, units), BF16),
            pltpu.VMEM((chans, units), BF16),
            pltpu.VMEM((units, 128), F32),
        ]
        + margin_scratch(slots, edge, chans),
    )
    cells = slots * edge * edge
    return pl.pallas_call(
        mlp_kernel,
        grid_spec=grid_spec,
        out_shape=[
            jax.ShapeDtypeStruct(state.shape, BF16),
            jax.ShapeDtypeStruct(state.shape, F32),
            jax.ShapeDtypeStruct((slots, 4, HALO, edge, chans), BF16),
            jax.ShapeDtypeStruct((units, chans), F32),
            jax.ShapeDtypeStruct((units, chans), F32),
            jax.ShapeDtypeStruct((units, 128), F32),
            jax.ShapeDtypeStruct((5, 8, chans), F32),
        ],
        compiler_params=params(VMEM_MIB),
        cost_estimate=pl.CostEstimate(
            flops=12 * cells * units * chans, bytes_accessed=14 * cells * chans, transcendentals=0
        ),
        name="mlp",
    )(slot, here, *sources, conv, state, cot, mask, weights, *par)


def tap_grad_kernel(slot_ref, here_ref, *refs):
    sources = refs[:5]
    state_ref, mask_ref, grad_ref, upacc, vec, out_ref = refs[5:11]
    padded, totals, small = refs[11:14]
    window, sem = refs[14:]
    tile, tiles = pl.program_id(0), pl.num_programs(0)
    edge, chans = grad_ref.shape[1], grad_ref.shape[3]

    @pl.when(tile == 0)
    def _():
        load_window(sources, window, sem)
        totals[...] = jnp.zeros_like(totals)
        zero_margins(padded)

    fill_masked(padded, state_ref, mask_ref)
    fill_margins(padded, window, slot_ref, here_ref, tile)

    for b in range(KSIZE):

        def body(n, sums, b=b):
            sums = list(sums)
            row = n * ROWS
            for g in range(edge // 8):
                grads = [grad_ref[0, row + i, g * 8 : g * 8 + 8] for i in range(ROWS)]
                for r in range(ROWS + KSIZE - 1):
                    cells = padded[row + r, pl.ds(g * 8 + b, 8), :]
                    for a in range(KSIZE):
                        if 0 <= r - a < ROWS:
                            sums[a] = sums[a] + cells * grads[r - a]
            return tuple(sums)

        start = tuple(totals[a * KSIZE + b] for a in range(KSIZE))
        sums = lax.fori_loop(0, edge // ROWS, body, start)
        for a in range(KSIZE):
            totals[a * KSIZE + b] = sums[a]

    @pl.when(tile == tiles - 1)
    def _():
        small[...] = jnp.zeros_like(small)
        small[0:TAPS] = jnp.sum(totals[...], 1)
        small[TAPS : TAPS + 5] = jnp.sum(vec[...], 1)
        units = upacc.shape[0]
        for u in range(units // 128):
            small[TAPS + 5 + u : TAPS + 6 + u] = jnp.sum(
                upacc[u * 128 : (u + 1) * 128].T, 0, keepdims=True
            )
        high = small[...].astype(BF16)
        out_ref[0] = high
        out_ref[1] = (small[...] - high.astype(F32)).astype(BF16)


def tap_grad_call(slot, here, sources, state, mask, grad, upacc, vec):
    slots, edge, _, chans = state.shape
    rows = TAPS + 5 + upacc.shape[0] // 128
    rows = -(-rows // 16) * 16
    tile_spec = pl.BlockSpec((1, edge, edge, chans), lambda s, *_: (s, 0, 0, 0))
    grid_spec = pltpu.PrefetchScalarGridSpec(
        num_scalar_prefetch=2,
        grid=(slots,),
        in_specs=[pl.BlockSpec(memory_space=pl.ANY)] * 5
        + [
            tile_spec,
            pl.BlockSpec((1, edge, edge), lambda s, *_: (s, 0, 0)),
            tile_spec,
            pl.BlockSpec(upacc.shape, lambda s, *_: (0, 0)),
            pl.BlockSpec(vec.shape, lambda s, *_: (0, 0, 0)),
        ],
        out_specs=pl.BlockSpec((2, rows, chans), lambda s, *_: (0, 0, 0)),
        scratch_shapes=[
            pltpu.VMEM(padded_shape(edge, chans), F32),
            pltpu.VMEM((TAPS, 8, chans), F32),
            pltpu.VMEM((rows, chans), F32),
        ]
        + window_scratch(slots, edge, chans),
    )
    return pl.pallas_call(
        tap_grad_kernel,
        grid_spec=grid_spec,
        out_shape=jax.ShapeDtypeStruct((2, rows, chans), BF16),
        compiler_params=params(VMEM_MIB),
        cost_estimate=conv_cost(slots, edge, chans),
        name="tap_grad",
    )(slot, here, *sources, state, mask, grad, upacc, vec)


def state_grad_kernel(slot_ref, here_ref, *refs):
    sources = refs[:5]
    grad_ref, cot_ref, mask_ref, weight_ref, out_ref, padded, conv_s, window, sem = refs[5:]
    tile = pl.program_id(0)
    edge, chans = grad_ref.shape[1], grad_ref.shape[3]

    @pl.when(tile == 0)
    def _():
        load_window(sources, window, sem)
        zero_margins(padded)

    def fill(n, carry):
        for r in range(8):
            i = n * 8 + r
            padded[HALO + i, HALO : HALO + edge] = grad_ref[0, i]
        return carry

    lax.fori_loop(0, edge // 8, fill, 0)
    fill_margins(padded, window, slot_ref, here_ref, tile)

    def body(n, carry):
        row = n * CONV_ROWS
        for g in range(edge // 8):

            def write(i, value):
                conv_s[i, g * 8 : g * 8 + 8] = value

            conv_rows(padded, weight_ref, row, g * 8, write, chans)
        for k in range(0, CONV_ROWS, 8):
            slabs = spread(mask_ref[0, pl.ds(pl.multiple_of(row + k, 8), 8)], chans)
            for r in range(8):
                i = row + k + r
                out_ref[0, i] = (cot_ref[0, i].astype(F32) + slabs[r] * conv_s[k + r]).astype(BF16)
        return carry

    lax.fori_loop(0, edge // CONV_ROWS, body, 0)


def state_grad_call(slot, here, sources, grad, cot, mask, weights):
    slots, edge, _, chans = cot.shape
    tile_spec = pl.BlockSpec((1, edge, edge, chans), lambda s, *_: (s, 0, 0, 0))
    grid_spec = pltpu.PrefetchScalarGridSpec(
        num_scalar_prefetch=2,
        grid=(slots,),
        in_specs=[pl.BlockSpec(memory_space=pl.ANY)] * 5
        + [
            tile_spec,
            tile_spec,
            pl.BlockSpec((1, edge, edge), lambda s, *_: (s, 0, 0)),
            pl.BlockSpec((TAPS, chans), lambda s, *_: (0, 0)),
        ],
        out_specs=tile_spec,
        scratch_shapes=[
            pltpu.VMEM(padded_shape(edge, chans), F32),
            pltpu.VMEM((CONV_ROWS, edge, chans), F32),
        ]
        + window_scratch(slots, edge, chans),
    )
    return pl.pallas_call(
        state_grad_kernel,
        grid_spec=grid_spec,
        out_shape=jax.ShapeDtypeStruct(cot.shape, BF16),
        compiler_params=params(VMEM_MIB),
        cost_estimate=conv_cost(slots, edge, chans),
        name="state_grad",
    )(slot, here, *sources, grad, cot, mask, weights)


def exchange(bands):
    return [
        bands if offset == 0 else shifted(bands, "tx", -offset)
        for offset in range(-REACH, REACH + 1)
    ]


def per_device(
    tile_state,
    cotangent,
    neighbours,
    land_mask,
    kernel,
    conv_bias,
    norm_gain,
    norm_bias,
    w_up,
    up_bias,
    w_down,
    down_bias,
    layer_scale,
):
    slots, edge, chans = (tile_state.shape[0], tile_state.shape[1], tile_state.shape[3])
    units = w_up.shape[0]
    count = lax.axis_size("tx")
    mask = land_mask.reshape(slots, edge, edge).astype(F32)
    first_slot = (lax.axis_index("tx") - REACH) * slots
    here = (neighbours >= 0).astype(jnp.int32)
    slot = jnp.clip(neighbours - first_slot, 0, (2 * REACH + 1) * slots - 1)
    par = (
        conv_bias[None],
        norm_gain[None],
        norm_bias[None],
        w_up,
        up_bias[None],
        w_down,
        down_bias[None],
        layer_scale[None],
    )
    flipped = kernel[::-1]

    window = exchange(bands_call(tile_state, mask))
    conv = own_conv_call(tile_state, mask, kernel)
    block_out, grad, grad_bands, gup, gdown, upacc, vec = mlp_call(
        slot, here, window, conv, tile_state, cotangent, mask, kernel, par
    )
    grad_window = exchange(grad_bands)

    small = tap_grad_call(slot, here, window, tile_state, mask, grad, upacc, vec)
    rows = small.shape[1]
    sums = small.reshape(2 * rows, chans)
    pieces = jnp.concatenate(
        [
            gup.astype(BF16).reshape(count, -1, chans),
            gdown.astype(BF16).reshape(count, -1, chans),
            jnp.broadcast_to(sums[None], (count,) + sums.shape),
        ],
        1,
    )
    pieces, grad_window, grad = lax.optimization_barrier((pieces, grad_window, grad))
    pieces = lax.all_to_all(pieces, "tx", 0, 0, tiled=True)
    totals = jnp.sum(pieces.astype(F32), 0)
    share = units // count
    grads = (totals[:share], totals[share : 2 * share])
    small = totals[2 * share : 2 * share + rows] + totals[2 * share + rows :]

    grad_state = state_grad_call(slot, here, grad_window, grad, cotangent, mask, flipped)

    grad_kernel = small[:TAPS]
    grad_vectors = small[TAPS : TAPS + 5]
    grad_up_bias = small[TAPS + 5 : TAPS + 5 + units // 128].reshape(units)
    return (block_out, grad_state, grads[0], grads[1], grad_kernel, grad_vectors, grad_up_bias)


def solution(mesh):
    tiles = P(("groups", "tx"), None, None, None)
    rows = P(("groups", "tx"), None)
    return jax.shard_map(
        per_device,
        mesh=mesh,
        in_specs=(tiles, tiles, rows, rows) + (P(),) * 9,
        out_specs=(tiles, tiles, rows, rows, P("groups", None), P("groups", None), P("groups")),
        check_vma=False,
    )
```

profile of v0, /device:TPU:0, one launch (start us, length us, event | category | flops | bytes accessed | tf_op | source)
XLA Modules:
  0.0 138.5 jit_solution(5544587174334512533)
XLA Ops:
  0.6 0.8 convert_element_type.18
  1.4 0.7 convert_element_type.19.mask_ref.refs_8_.refs_6_.refs_7_
  2.1 2.5 %bands.1.refs_2_ = bf16[2,4,3,64,128]{4,3,2,1,0:T(8,128)(2,1)} custom-call(bf16[2,64,64,128]{3,2,1,0:T(8,128)(2,1)} %refs_5_.1, f32[2,64,64]{2,1,0:T(8,128)} %convert_element_type.19.mask_ref.refs_8_.refs_6_.refs_7_), custom_call_target="tpu_custom_call" | custom-call | tf_op jit(solution)/shard_map/bands/pallas_call | solution.py:72
  4.7 4.9 %collective-permute-start = (bf16[2,4,3,64,128]{4,3,2,1,0:T(8,128)(2,1)}, bf16[2,4,3,64,128]{4,3,2,1,0:T(8,128)(2,1)S(1)}, u32[]{:S(2)}, u32[]{:S(2)}) collective-permute-start(bf16[2,4,3,64,128]{4,3,2,1,0:T(8,128)(2,1)} %bands.1.refs_2_), channel_id=1, source_target_pairs={{0,2},{1,3},{2,4},{3,5},{4,6},{5,7},{6,8},{7,9},{8,10},{9,11},{10,... | collective-permute-start | bytes 1179656 | tf_op jit(solution)/shard_map/ppermute | solution.py:34
  9.5 1.5 %collective-permute-start.1 = (bf16[2,4,3,64,128]{4,3,2,1,0:T(8,128)(2,1)}, bf16[2,4,3,64,128]{4,3,2,1,0:T(8,128)(2,1)S(1)}, u32[]{:S(2)}, u32[]{:S(2)}) collective-permute-start(bf16[2,4,3,64,128]{4,3,2,1,0:T(8,128)(2,1)} %bands.1.refs_2_), channel_id=1, source_target_pairs={{0,1},{1,2},{2,3},{3,4},{4,5},{5,6},{6,7},{7,8},{8,9},{9,10},{10,1... | collective-permute-start | bytes 1179656 | tf_op jit(solution)/shard_map/ppermute | solution.py:34
  11.0 1.3 collective-permute-start.2
  12.3 1.3 collective-permute-start.3
  13.6 0.0 copy-start.9
  13.6 18.5 %own_conv.1.refs_5_ = f32[2,64,64,128]{3,2,1,0:T(8,128)} custom-call(bf16[2,64,64,128]{3,2,1,0:T(8,128)(2,1)} %refs_5_.1, f32[2,64,64]{2,1,0:T(8,128)} %convert_element_type.19.mask_ref.refs_8_.refs_6_.refs_7_, f32[49,128]{1,0:T(8,128)} %refs_9_.1), custom_call_target="tpu_custom_call" | custom-call | flops 102760448 | bytes 8388608 | tf_op jit(solution)/shard_map/own_conv/pallas_call | solution.py:164
  32.2 0.0 copy-done.9
  32.2 0.6 compare_convert_fusion.here_ref
  32.8 0.6 subtract_clamp_fusion.slot_ref
  33.3 0.0 collective-permute-done.refs_0_
  33.3 0.0 copy-start
  33.3 0.0 collective-permute-done.1.refs_1_
  33.3 0.0 copy-start.1
  33.3 0.0 collective-permute-done.2.refs_3_
  33.3 0.0 copy-start.2
  33.4 0.0 collective-permute-done.3.refs_4_
  33.4 0.0 copy-start.3
  33.4 0.7 copy-done
  34.1 0.1 copy-done.1
  34.2 0.1 copy-done.2
  34.4 0.1 copy-done.3
  34.5 32.2 %mlp.1 = (bf16[2,64,64,128]{3,2,1,0:T(8,128)(2,1)}, f32[2,64,64,128]{3,2,1,0:T(8,128)}, bf16[2,4,3,64,128]{4,3,2,1,0:T(8,128)(2,1)}, f32[512,128]{1,0:T(8,128)},...) custom-call(s32[2,8]{1,0:T(2,128)} %subtract_clamp_fusion.slot_ref, ...), custom_call_target="tpu_custom_call" | custom-call | flops 6442450944 | bytes 14680064 | tf_op jit(solution)/shard_map/mlp/pallas_call | solution.py:499
  66.7 6.9 %collective-permute-start.4 = (bf16[2,4,3,64,128]{4,3,2,1,0:T(8,128)(2,1)}, bf16[2,4,3,64,128]{4,3,2,1,0:T(8,128)(2,1)S(1)}, u32[]{:S(2)}, u32[]{:S(2)}) collective-permute-start(bf16[2,4,3,64,128]{4,3,2,1,0:T(8,128)(2,1)} %get-tuple-element.30.refs_2_), channel_id=1, source_target_pairs={{0,2},{1,3},{2,4},{3,5},{4,6},{5,7},{6,8},{7,9},{8,10},{9,11},{10,... | collective-permute-start | bytes 1179656 | tf_op jit(solution)/shard_map/ppermute | solution.py:34
  73.6 1.8 %collective-permute-start.5 = (bf16[2,4,3,64,128]{4,3,2,1,0:T(8,128)(2,1)}, bf16[2,4,3,64,128]{4,3,2,1,0:T(8,128)(2,1)S(1)}, u32[]{:S(2)}, u32[]{:S(2)}) collective-permute-start(bf16[2,4,3,64,128]{4,3,2,1,0:T(8,128)(2,1)} %get-tuple-element.30.refs_2_), channel_id=1, source_target_pairs={{0,1},{1,2},{2,3},{3,4},{4,5},{5,6},{6,7},{7,8},{8,9},{9,10},{10,1... | collective-permute-start | bytes 1179656 | tf_op jit(solution)/shard_map/ppermute | solution.py:34
  75.3 1.3 collective-permute-start.6
  76.6 1.3 collective-permute-start.7
  77.9 1.0 convert_element_type.20
  78.9 1.0 convert_element_type.21
  79.9 21.3 %tap_grad.1 = bf16[2,64,128]{2,1,0:T(8,128)(2,1)} custom-call(s32[2,8]{1,0:T(2,128)} %subtract_clamp_fusion.slot_ref, s32[2,8]{1,0:T(2,128)} %compare_convert_fusion.here_ref, bf16[2,4,3,64,128]{4,3,2,1,0:T(8,128)(2,1)} %copy-done, bf16[2,4,3,64,128]{4,3,2,1,0:T(8,128)(2,1)} %copy-done.1, bf16[2,4,3,64,128]{4,3,2,1,0:T(8,128)(2,1)} %bands.1.refs_2_, ...), custom_call_target="tpu_custom_call" | custom-call | flops 102760448 | bytes 8388608 | tf_op jit(solution)/shard_map/tap_grad/pallas_call | solution.py:594
  101.2 0.0 copy-start.8
  101.2 0.9 broadcast_in_dim.32
  102.1 1.0 pad_maximum_fusion
  103.0 0.0 collective-permute-done.4.refs_0_
  103.0 0.0 copy-start.4
  103.0 0.0 collective-permute-done.5.refs_1_
  103.0 0.0 copy-start.5
  103.1 0.0 collective-permute-done.6.refs_3_
  103.1 0.0 copy-start.6
  103.1 0.0 collective-permute-done.7.refs_4_
  103.1 0.0 copy-start.7
  103.1 11.9 %all-to-all-start = ((bf16[16,192,128]{2,1,0:T(8,128)(2,1)}), bf16[16,192,128]{2,1,0:T(8,128)(2,1)S(1)}, u32[]{:S(2)}, u32[]{:S(2)}) async-start(bf16[16,192,128]{2,1,0:T(8,128)(2,1)} %pad_maximum_fusion), calls=%async_computation | async-start | bytes 1572864 | tf_op jit(solution)/shard_map/all_to_all | solution.py:732
  115.0 0.0 copy-done.8
  115.0 0.6 rev.3.refs_8_
  115.6 0.0 copy-done.4
  115.6 0.0 copy-done.5
  115.6 0.0 copy-done.6
  115.6 0.0 copy-done.7
  115.6 20.3 %state_grad.1 = bf16[2,64,64,128]{3,2,1,0:T(8,128)(2,1)} custom-call(s32[2,8]{1,0:T(2,128)} %subtract_clamp_fusion.slot_ref, s32[2,8]{1,0:T(2,128)} %compare_convert_fusion.here_ref, bf16[2,4,3,64,128]{4,3,2,1,0:T(8,128)(2,1)} %copy-done.4, bf16[2,4,3,64,128]{4,3,2,1,0:T(8,128)(2,1)} %copy-done.5, bf16[2,4,3,64,128]{4,3,2,1,0:T(8,128)(2,1)} %get-tuple-element.30.refs_2_, ...), custom_call_target="tpu_custom_call" | custom-call | flops 102760448 | bytes 8388608 | tf_op jit(solution)/shard_map/state_grad/pallas_call | solution.py:662
  135.9 0.0 all-to-all-done
  136.0 0.1 convert_reduce_fusion
  136.1 0.6 slice.32
  136.7 0.6 slice.33
  137.3 0.6 slice_bitcast_fusion
  137.9 0.6 fusion
  (1 shorter events, 0.0 us)
Async XLA Ops:
  4.7 28.6 %collective-permute-start = (bf16[2,4,3,64,128]{4,3,2,1,0:T(8,128)(2,1)}, bf16[2,4,3,64,128]{4,3,2,1,0:T(8,128)(2,1)S(1)}, u32[]{:S(2)}, u32[]{:S(2)}) collective-permute-start(bf16[2,4,3,64,128]{4,3,2,1,0:T(8,128)(2,1)} %bands.1.refs_2_), channel_id=1, source_target_pairs={{0,2},{1,3},{2,4},{3,5},{4,6},{5,7},{6,8},{7,9},{8,10},{9,11},{10,... | collective-permute-start | bytes 1179656 | tf_op jit(solution)/shard_map/ppermute | solution.py:34
  9.5 23.8 %collective-permute-start.1 = (bf16[2,4,3,64,128]{4,3,2,1,0:T(8,128)(2,1)}, bf16[2,4,3,64,128]{4,3,2,1,0:T(8,128)(2,1)S(1)}, u32[]{:S(2)}, u32[]{:S(2)}) collective-permute-start(bf16[2,4,3,64,128]{4,3,2,1,0:T(8,128)(2,1)} %bands.1.refs_2_), channel_id=1, source_target_pairs={{0,1},{1,2},{2,3},{3,4},{4,5},{5,6},{6,7},{7,8},{8,9},{9,10},{10,1... | collective-permute-start | bytes 1179656 | tf_op jit(solution)/shard_map/ppermute | solution.py:34
  11.0 22.3 %collective-permute-start.2 = (bf16[2,4,3,64,128]{4,3,2,1,0:T(8,128)(2,1)}, bf16[2,4,3,64,128]{4,3,2,1,0:T(8,128)(2,1)S(1)}, u32[]{:S(2)}, u32[]{:S(2)}) collective-permute-start(bf16[2,4,3,64,128]{4,3,2,1,0:T(8,128)(2,1)} %bands.1.refs_2_), channel_id=1, source_target_pairs={{1,0},{2,1},{3,2},{4,3},{5,4},{6,5},{7,6},{8,7},{9,8},{10,9},{11,1... | collective-permute-start | bytes 1179656 | tf_op jit(solution)/shard_map/ppermute | solution.py:34
  12.3 21.0 %collective-permute-start.3 = (bf16[2,4,3,64,128]{4,3,2,1,0:T(8,128)(2,1)}, bf16[2,4,3,64,128]{4,3,2,1,0:T(8,128)(2,1)S(1)}, u32[]{:S(2)}, u32[]{:S(2)}) collective-permute-start(bf16[2,4,3,64,128]{4,3,2,1,0:T(8,128)(2,1)} %bands.1.refs_2_), channel_id=1, source_target_pairs={{2,0},{3,1},{4,2},{5,3},{6,4},{7,5},{8,6},{9,7},{10,8},{11,9},{12,... | collective-permute-start | bytes 1179656 | tf_op jit(solution)/shard_map/ppermute | solution.py:34
  13.6 18.6 %copy-start.9 = (s32[2,8]{1,0:T(2,128)S(1)}, s32[2,8]{1,0:T(2,128)}, u32[]{:S(2)}) copy-start(s32[2,8]{1,0:T(2,128)} %param.15) | copy-start | bytes 196
  33.3 0.8 copy-start
  33.3 0.9 copy-start.1
  33.3 1.0 copy-start.2
  33.4 1.1 copy-start.3
  66.7 36.4 %collective-permute-start.4 = (bf16[2,4,3,64,128]{4,3,2,1,0:T(8,128)(2,1)}, bf16[2,4,3,64,128]{4,3,2,1,0:T(8,128)(2,1)S(1)}, u32[]{:S(2)}, u32[]{:S(2)}) collective-permute-start(bf16[2,4,3,64,128]{4,3,2,1,0:T(8,128)(2,1)} %get-tuple-element.30.refs_2_), channel_id=1, source_target_pairs={{0,2},{1,3},{2,4},{3,5},{4,6},{5,7},{6,8},{7,9},{8,10},{9,11},{10,... | collective-permute-start | bytes 1179656 | tf_op jit(solution)/shard_map/ppermute | solution.py:34
  73.6 29.5 %collective-permute-start.5 = (bf16[2,4,3,64,128]{4,3,2,1,0:T(8,128)(2,1)}, bf16[2,4,3,64,128]{4,3,2,1,0:T(8,128)(2,1)S(1)}, u32[]{:S(2)}, u32[]{:S(2)}) collective-permute-start(bf16[2,4,3,64,128]{4,3,2,1,0:T(8,128)(2,1)} %get-tuple-element.30.refs_2_), channel_id=1, source_target_pairs={{0,1},{1,2},{2,3},{3,4},{4,5},{5,6},{6,7},{7,8},{8,9},{9,10},{10,1... | collective-permute-start | bytes 1179656 | tf_op jit(solution)/shard_map/ppermute | solution.py:34
  75.3 27.7 %collective-permute-start.6 = (bf16[2,4,3,64,128]{4,3,2,1,0:T(8,128)(2,1)}, bf16[2,4,3,64,128]{4,3,2,1,0:T(8,128)(2,1)S(1)}, u32[]{:S(2)}, u32[]{:S(2)}) collective-permute-start(bf16[2,4,3,64,128]{4,3,2,1,0:T(8,128)(2,1)} %get-tuple-element.30.refs_2_), channel_id=1, source_target_pairs={{1,0},{2,1},{3,2},{4,3},{5,4},{6,5},{7,6},{8,7},{9,8},{10,9},{11,1... | collective-permute-start | bytes 1179656 | tf_op jit(solution)/shard_map/ppermute | solution.py:34
  76.6 26.5 %collective-permute-start.7 = (bf16[2,4,3,64,128]{4,3,2,1,0:T(8,128)(2,1)}, bf16[2,4,3,64,128]{4,3,2,1,0:T(8,128)(2,1)S(1)}, u32[]{:S(2)}, u32[]{:S(2)}) collective-permute-start(bf16[2,4,3,64,128]{4,3,2,1,0:T(8,128)(2,1)} %get-tuple-element.30.refs_2_), channel_id=1, source_target_pairs={{2,0},{3,1},{4,2},{5,3},{6,4},{7,5},{8,6},{9,7},{10,8},{11,9},{12,... | collective-permute-start | bytes 1179656 | tf_op jit(solution)/shard_map/ppermute | solution.py:34
  101.2 13.8 %copy-start.8 = (f32[49,128]{1,0:T(8,128)S(1)}, f32[49,128]{1,0:T(8,128)}, u32[]{:S(2)}) copy-start(f32[49,128]{1,0:T(8,128)} %refs_9_.1) | copy-start | bytes 75268
  103.0 12.6 %copy-start.4 = (bf16[2,4,3,64,128]{4,3,2,1,0:T(8,128)(2,1)}, bf16[2,4,3,64,128]{4,3,2,1,0:T(8,128)(2,1)S(1)}, u32[]{:S(2)}) copy-start(bf16[2,4,3,64,128]{4,3,2,1,0:T(8,128)(2,1)S(1)} %collective-permute-done.4.refs_0_) | copy-start | bytes 1179652
  103.0 12.6 %copy-start.5 = (bf16[2,4,3,64,128]{4,3,2,1,0:T(8,128)(2,1)}, bf16[2,4,3,64,128]{4,3,2,1,0:T(8,128)(2,1)S(1)}, u32[]{:S(2)}) copy-start(bf16[2,4,3,64,128]{4,3,2,1,0:T(8,128)(2,1)S(1)} %collective-permute-done.5.refs_1_) | copy-start | bytes 1179652
  103.1 12.5 %copy-start.6 = (bf16[2,4,3,64,128]{4,3,2,1,0:T(8,128)(2,1)}, bf16[2,4,3,64,128]{4,3,2,1,0:T(8,128)(2,1)S(1)}, u32[]{:S(2)}) copy-start(bf16[2,4,3,64,128]{4,3,2,1,0:T(8,128)(2,1)S(1)} %collective-permute-done.6.refs_3_) | copy-start | bytes 1179652
  103.1 12.5 %copy-start.7 = (bf16[2,4,3,64,128]{4,3,2,1,0:T(8,128)(2,1)}, bf16[2,4,3,64,128]{4,3,2,1,0:T(8,128)(2,1)S(1)}, u32[]{:S(2)}) copy-start(bf16[2,4,3,64,128]{4,3,2,1,0:T(8,128)(2,1)S(1)} %collective-permute-done.7.refs_4_) | copy-start | bytes 1179652
  103.1 32.8 %all-to-all-start = ((bf16[16,192,128]{2,1,0:T(8,128)(2,1)}), bf16[16,192,128]{2,1,0:T(8,128)(2,1)S(1)}, u32[]{:S(2)}, u32[]{:S(2)}) async-start(bf16[16,192,128]{2,1,0:T(8,128)(2,1)} %pad_maximum_fusion), calls=%async_computation | async-start | bytes 1572864 | tf_op jit(solution)/shard_map/all_to_all | solution.py:732
where the time goes:
time: 139 us; the launch traced here: 138 us
  Pallas kernels  94.9 us (68%)
  starting transfers between devices  32 us (23%)
  local copies, waits for them, and re-layouts  5.73 us (4%)
  other arithmetic  4.91 us (4%)
    pallas_call x1, Pallas kernels, mlp_call(): pl.pallas_call(mlp_kernel, grid_spec=grid_spec, out_shape=[jax.ShapeDtype...  32.2 us
    pallas_call x1, Pallas kernels, tap_grad_call(): pl.pallas_call(tap_grad_kernel, grid_spec=grid_spec, out_shape=jax.ShapeD...  21.3 us
    pallas_call x1, Pallas kernels, state_grad_call(): pl.pallas_call(state_grad_kernel, grid_spec=grid_spec, out_shape=jax.Shap...  20.3 us
    ppermute x8, starting transfers between devices, shifted(): return lax.ppermute(shard, axis, pairs)  20.1 us
    pallas_call x1, Pallas kernels, own_conv_call(): pl.pallas_call(own_conv_kernel, grid=(slots,), in_specs=[pl.BlockSpec((1,...  18.5 us
    all_to_all x1, starting transfers between devices, per_device(): pieces = lax.all_to_all(pieces, 'tx', 0, 0, tiled=True)  11.9 us
  transfers between devices with their start and end apart: 9, of which 0 were waited for; matrix products, arithmetic and copies ran while one was open for 4% of the time, Pallas kernels for 43%

commit v1 on v0

--- a/solution.py
+++ b/solution.py
@@ -43,15 +43,15 @@
     row = lax.broadcasted_iota(jnp.int32, (height, height * chans), 0)
     lane = lax.broadcasted_iota(jnp.int32, (height, height * chans), 1)
     pick = ((lane >= row * chans) & (lane < (row + 1) * chans)).astype(F32).astype(BF16)
-    wide = jnp.dot(rows.T.astype(BF16), pick, preferred_element_type=F32)
+    wide = jnp.dot(rows.astype(F32).T.astype(BF16), pick, preferred_element_type=F32)
     return [wide[:, r * chans : (r + 1) * chans] for r in range(height)]
 
 
 def bands_kernel(state_ref, mask_ref, out_ref, left, right):
     edge = state_ref.shape[1]
     low = edge - HALO
-    upper = mask_ref[0, 0:8].T
-    lower = mask_ref[0, edge - 8 :].T
+    upper = mask_ref[0, 0:8].astype(F32).T
+    lower = mask_ref[0, edge - 8 :].astype(F32).T
     for q in range(HALO):
         out_ref[0, 0, q] = (state_ref[0, q].astype(F32) * upper[:, q : q + 1]).astype(BF16)
         p = 8 - HALO + q
@@ -60,10 +60,11 @@
     right[...] = state_ref[0, :, edge - 16 :].astype(F32).reshape(right.shape)
     for q in range(HALO):
         out_ref[0, 2, q] = (
-            left[pl.ds(q, edge, stride=16), :] * mask_ref[0, :, q : q + 1]
+            left[pl.ds(q, edge, stride=16), :] * mask_ref[0, :, q : q + 1].astype(F32)
         ).astype(BF16)
         out_ref[0, 3, q] = (
-            right[pl.ds(16 - HALO + q, edge, stride=16), :] * mask_ref[0, :, low + q : low + q + 1]
+            right[pl.ds(16 - HALO + q, edge, stride=16), :]
+            * mask_ref[0, :, low + q : low + q + 1].astype(F32)
         ).astype(BF16)
 
 
@@ -88,10 +89,11 @@
     return jnp.broadcast_to(weight_ref[index : index + 1, :], (8, chans))
 
 
-def conv_rows(padded, weight_ref, row, column, write, chans):
+def conv_rows(padded, weight_ref, row, column, write, chans, flip=False):
     totals = [None] * CONV_ROWS
     for b in range(KSIZE):
-        weights = [tap(weight_ref, a * KSIZE + b, chans) for a in range(KSIZE)]
+        taps = [a * KSIZE + b for a in range(KSIZE)]
+        weights = [tap(weight_ref, TAPS - 1 - t if flip else t, chans) for t in taps]
         for r in range(CONV_ROWS + KSIZE - 1):
             cells = padded[row + r, pl.ds(column + b, 8), :]
             for a in range(KSIZE):
@@ -129,8 +131,8 @@
     lax.fori_loop(0, edge // 8, body, 0, unroll=4)
 
 
-def conv_tile(padded, weight_ref, out_ref):
-    edge, chans = out_ref.shape[1], out_ref.shape[3]
+def conv_tile(padded, weight_ref, out_ref, base):
+    height, edge, chans = out_ref.shape[1:]
 
     def body(n, carry):
         for g in range(edge // 8):
@@ -138,16 +140,21 @@
             def write(i, value):
                 out_ref[0, n * CONV_ROWS + i, g * 8 : g * 8 + 8] = value
 
-            conv_rows(padded, weight_ref, n * CONV_ROWS, g * 8, write, chans)
+            conv_rows(padded, weight_ref, base + n * CONV_ROWS, g * 8, write, chans)
         return carry
 
-    lax.fori_loop(0, edge // CONV_ROWS, body, 0)
+    lax.fori_loop(0, height // CONV_ROWS, body, 0)
 
 
 def own_conv_kernel(state_ref, mask_ref, weight_ref, out_ref, padded):
-    zero_margins(padded)
-    fill_masked(padded, state_ref, mask_ref)
-    conv_tile(padded, weight_ref, out_ref)
+    block = pl.program_id(1)
+
+    @pl.when(block == 0)
+    def _():
+        zero_margins(padded)
+        fill_masked(padded, state_ref, mask_ref)
+
+    conv_tile(padded, weight_ref, out_ref, block * out_ref.shape[1])
 
 
 def padded_shape(edge, chans):
@@ -163,13 +170,13 @@
     slots, edge, _, chans = state.shape
     return pl.pallas_call(
         own_conv_kernel,
-        grid=(slots,),
+        grid=(slots, edge // STEP_ROWS),
         in_specs=[
-            pl.BlockSpec((1, edge, edge, chans), lambda s: (s, 0, 0, 0)),
-            pl.BlockSpec((1, edge, edge), lambda s: (s, 0, 0)),
-            pl.BlockSpec((TAPS, chans), lambda s: (0, 0)),
+            pl.BlockSpec((1, edge, edge, chans), lambda s, n: (s, 0, 0, 0)),
+            pl.BlockSpec((1, edge, edge), lambda s, n: (s, 0, 0)),
+            pl.BlockSpec((TAPS, chans), lambda s, n: (0, 0)),
         ],
-        out_specs=pl.BlockSpec((1, edge, edge, chans), lambda s: (s, 0, 0, 0)),
+        out_specs=pl.BlockSpec((1, STEP_ROWS, edge, chans), lambda s, n: (s, n, 0, 0)),
         out_shape=jax.ShapeDtypeStruct((slots, edge, edge, chans), F32),
         scratch_shapes=[pltpu.VMEM(padded_shape(edge, chans), F32)],
         compiler_params=params(VMEM_MIB),
@@ -178,15 +185,21 @@
     )(state, mask, weights)
 
 
-def load_window(sources, window, sem):
+def window_copies(sources, window, sem):
     slots = sources[0].shape[0]
-    copies = [
+    return [
         pltpu.make_async_copy(source, window.at[pl.ds(k * slots, slots)], sem.at[k])
         for k, source in enumerate(sources)
     ]
-    for copy in copies:
+
+
+def start_window(sources, window, sem):
+    for copy in window_copies(sources, window, sem):
         copy.start()
-    for copy in copies:
+
+
+def wait_window(sources, window, sem):
+    for copy in window_copies(sources, window, sem):
         copy.wait()
 
 
@@ -301,8 +314,8 @@
 
     @pl.when((tile == 0) & (block == 0))
     def _():
-        load_window(sources, window, sem)
         clear_margins(north, south, west, east)
+        wait_window(sources, window, sem)
 
     @pl.when(block == 0)
     def _():
@@ -319,7 +332,7 @@
         add_columns(west, east, weight_ref, block * height + n * ROWS, target, n * ROWS, chans)
         return carry
 
-    lax.fori_loop(0, height // ROWS, body, 0)
+    lax.fori_loop(0, height // ROWS, body, 0, unroll=True)
 
     @pl.when(block == 0)
     def _():
@@ -408,6 +421,7 @@
 
     @pl.when((tile == 0) & (block == 0))
     def _():
+        start_window(sources, scratch[0], scratch[1])
         for ref in (gup, gdown, upacc, vec):
             ref[...] = jnp.zeros_like(ref)
         wup_t[...] = wup[...].astype(F32).T.astype(BF16)
@@ -445,7 +459,7 @@
             tile_grad[pl.ds(start, CELLS), :] = dconv
         return carry
 
-    lax.fori_loop(0, height // ROWS, body, 0)
+    lax.fori_loop(0, height // ROWS, body, 0, unroll=True)
 
     @pl.when(block == blocks - 1)
     def _():
@@ -518,19 +532,24 @@
 
 def tap_grad_kernel(slot_ref, here_ref, *refs):
     sources = refs[:5]
-    state_ref, mask_ref, grad_ref, upacc, vec, out_ref = refs[5:11]
-    padded, totals, small = refs[11:14]
-    window, sem = refs[14:]
+    state_ref, mask_ref, grad_ref, gup, gdown, upacc, vec, out_ref = refs[5:13]
+    padded, totals, small = refs[13:16]
+    window, sem = refs[16:]
     tile, tiles = pl.program_id(0), pl.num_programs(0)
     edge, chans = grad_ref.shape[1], grad_ref.shape[3]
 
     @pl.when(tile == 0)
     def _():
-        load_window(sources, window, sem)
+        start_window(sources, window, sem)
         totals[...] = jnp.zeros_like(totals)
         zero_margins(padded)
 
     fill_masked(padded, state_ref, mask_ref)
+
+    @pl.when(tile == 0)
+    def _():
+        wait_window(sources, window, sem)
+
     fill_margins(padded, window, slot_ref, here_ref, tile)
 
     for b in range(KSIZE):
@@ -563,14 +582,22 @@
                 upacc[u * 128 : (u + 1) * 128].T, 0, keepdims=True
             )
         high = small[...].astype(BF16)
-        out_ref[0] = high
-        out_ref[1] = (small[...] - high.astype(F32)).astype(BF16)
-
-
-def tap_grad_call(slot, here, sources, state, mask, grad, upacc, vec):
+        rest = (small[...] - high.astype(F32)).astype(BF16)
+        count, rows = out_ref.shape[0], small.shape[0]
+        share = units // count
+        for d in range(count):
+            part = slice(d * share, (d + 1) * share)
+            out_ref[d, 0:share] = gup[part].astype(BF16)
+            out_ref[d, share : 2 * share] = gdown[part].astype(BF16)
+            out_ref[d, 2 * share : 2 * share + rows] = high
+            out_ref[d, 2 * share + rows :] = rest
+
+
+def tap_grad_call(slot, here, sources, state, mask, grad, gup, gdown, upacc, vec, count):
     slots, edge, _, chans = state.shape
     rows = TAPS + 5 + upacc.shape[0] // 128
     rows = -(-rows // 16) * 16
+    length = 2 * (upacc.shape[0] // count) + 2 * rows
     tile_spec = pl.BlockSpec((1, edge, edge, chans), lambda s, *_: (s, 0, 0, 0))
     grid_spec = pltpu.PrefetchScalarGridSpec(
         num_scalar_prefetch=2,
@@ -580,10 +607,12 @@
             tile_spec,
             pl.BlockSpec((1, edge, edge), lambda s, *_: (s, 0, 0)),
             tile_spec,
+            pl.BlockSpec(gup.shape, lambda s, *_: (0, 0)),
+            pl.BlockSpec(gdown.shape, lambda s, *_: (0, 0)),
             pl.BlockSpec(upacc.shape, lambda s, *_: (0, 0)),
             pl.BlockSpec(vec.shape, lambda s, *_: (0, 0, 0)),
         ],
-        out_specs=pl.BlockSpec((2, rows, chans), lambda s, *_: (0, 0, 0)),
+        out_specs=pl.BlockSpec((count, length, chans), lambda s, *_: (0, 0, 0)),
         scratch_shapes=[
             pltpu.VMEM(padded_shape(edge, chans), F32),
             pltpu.VMEM((TAPS, 8, chans), F32),
@@ -594,11 +623,11 @@
     return pl.pallas_call(
         tap_grad_kernel,
         grid_spec=grid_spec,
-        out_shape=jax.ShapeDtypeStruct((2, rows, chans), BF16),
+        out_shape=jax.ShapeDtypeStruct((count, length, chans), BF16),
         compiler_params=params(VMEM_MIB),
         cost_estimate=conv_cost(slots, edge, chans),
         name="tap_grad",
-    )(slot, here, *sources, state, mask, grad, upacc, vec)
+    )(slot, here, *sources, state, mask, grad, gup, gdown, upacc, vec)
 
 
 def state_grad_kernel(slot_ref, here_ref, *refs):
@@ -609,7 +638,7 @@
 
     @pl.when(tile == 0)
     def _():
-        load_window(sources, window, sem)
+        start_window(sources, window, sem)
         zero_margins(padded)
 
     def fill(n, carry):
@@ -619,6 +648,11 @@
         return carry
 
     lax.fori_loop(0, edge // 8, fill, 0)
+
+    @pl.when(tile == 0)
+    def _():
+        wait_window(sources, window, sem)
+
     fill_margins(padded, window, slot_ref, here_ref, tile)
 
     def body(n, carry):
@@ -628,7 +662,7 @@
             def write(i, value):
                 conv_s[i, g * 8 : g * 8 + 8] = value
 
-            conv_rows(padded, weight_ref, row, g * 8, write, chans)
+            conv_rows(padded, weight_ref, row, g * 8, write, chans, True)
         for k in range(0, CONV_ROWS, 8):
             slabs = spread(mask_ref[0, pl.ds(pl.multiple_of(row + k, 8), 8)], chans)
             for r in range(8):
@@ -669,11 +703,55 @@
     )(slot, here, *sources, grad, cot, mask, weights)
 
 
-def exchange(bands):
-    return [
-        bands if offset == 0 else shifted(bands, "tx", -offset)
-        for offset in range(-REACH, REACH + 1)
-    ]
+def total_kernel(pieces_ref, up_ref, down_ref, taps_ref, vec_ref, bias_ref):
+    share = up_ref.shape[0]
+    rows = (pieces_ref.shape[1] - 2 * share) // 2
+    total = pieces_ref[0].astype(F32)
+    for d in range(1, pieces_ref.shape[0]):
+        total = total + pieces_ref[d].astype(F32)
+    up_ref[...] = total[:share]
+    down_ref[...] = total[share : 2 * share]
+    small = total[2 * share : 2 * share + rows] + total[2 * share + rows :]
+    taps_ref[...] = small[:TAPS]
+    vec_ref[...] = small[TAPS : TAPS + 5]
+    bias_ref[...] = small[TAPS + 5 : TAPS + 5 + bias_ref.shape[0]]
+
+
+def total_call(pieces, units):
+    count, _, chans = pieces.shape
+    share = units // count
+    shapes = [(share, chans), (share, chans), (TAPS, chans), (5, chans), (units // chans, chans)]
+    return pl.pallas_call(
+        total_kernel,
+        out_shape=[jax.ShapeDtypeStruct(shape, F32) for shape in shapes],
+        compiler_params=params(VMEM_MIB),
+        name="total",
+    )(pieces)
+
+
+def pair_pairs():
+    return [(i, i ^ 1) for i in range(lax.axis_size("tx"))]
+
+
+def direct(bands):
+    return (
+        shifted(bands, "tx", 2),
+        lax.ppermute(bands, "tx", pair_pairs()),
+        shifted(bands, "tx", -2),
+    )
+
+
+def relayed(below, above):
+    odd = lax.axis_index("tx") % 2 == 1
+    return lax.ppermute(jnp.where(odd, below, above), "tx", pair_pairs())
+
+
+def window_slots(neighbours, slots):
+    me = lax.axis_index("tx")
+    low = (me - REACH) * slots
+    slot = jnp.clip(neighbours - low, 0, (2 * REACH + 1) * slots - 1)
+    swap = (me % 2 == 1) & ((slot // slots == 1) | (slot // slots == 3))
+    return jnp.where(swap, slot + jnp.where(slot // slots == 1, 2, -2) * slots, slot)
 
 
 def per_device(
@@ -694,10 +772,9 @@
     slots, edge, chans = (tile_state.shape[0], tile_state.shape[1], tile_state.shape[3])
     units = w_up.shape[0]
     count = lax.axis_size("tx")
-    mask = land_mask.reshape(slots, edge, edge).astype(F32)
-    first_slot = (lax.axis_index("tx") - REACH) * slots
+    mask = land_mask.reshape(slots, edge, edge)
     here = (neighbours >= 0).astype(jnp.int32)
-    slot = jnp.clip(neighbours - first_slot, 0, (2 * REACH + 1) * slots - 1)
+    slot = window_slots(neighbours, slots)
     par = (
         conv_bias[None],
         norm_gain[None],
@@ -708,39 +785,29 @@
         down_bias[None],
         layer_scale[None],
     )
-    flipped = kernel[::-1]
-
-    window = exchange(bands_call(tile_state, mask))
+
+    bands = bands_call(tile_state, mask)
+    below, partner, above = direct(bands)
+    window = [below, relayed(below, above), bands, partner, above]
     conv = own_conv_call(tile_state, mask, kernel)
     block_out, grad, grad_bands, gup, gdown, upacc, vec = mlp_call(
         slot, here, window, conv, tile_state, cotangent, mask, kernel, par
     )
-    grad_window = exchange(grad_bands)
-
-    small = tap_grad_call(slot, here, window, tile_state, mask, grad, upacc, vec)
-    rows = small.shape[1]
-    sums = small.reshape(2 * rows, chans)
-    pieces = jnp.concatenate(
-        [
-            gup.astype(BF16).reshape(count, -1, chans),
-            gdown.astype(BF16).reshape(count, -1, chans),
-            jnp.broadcast_to(sums[None], (count,) + sums.shape),
-        ],
-        1,
+    below, partner, above = direct(grad_bands)
+
+    pieces = tap_grad_call(
+        slot, here, window, tile_state, mask, grad, gup, gdown, upacc, vec, count
     )
-    pieces, grad_window, grad = lax.optimization_barrier((pieces, grad_window, grad))
+    pieces, below, above, grad = lax.optimization_barrier((pieces, below, above, grad))
+    relay = relayed(below, above)
+    pieces, relay, grad = lax.optimization_barrier((pieces, relay, grad))
+    grad_window = [below, relay, grad_bands, partner, above]
     pieces = lax.all_to_all(pieces, "tx", 0, 0, tiled=True)
-    totals = jnp.sum(pieces.astype(F32), 0)
-    share = units // count
-    grads = (totals[:share], totals[share : 2 * share])
-    small = totals[2 * share : 2 * share + rows] + totals[2 * share + rows :]
-
-    grad_state = state_grad_call(slot, here, grad_window, grad, cotangent, mask, flipped)
-
-    grad_kernel = small[:TAPS]
-    grad_vectors = small[TAPS : TAPS + 5]
-    grad_up_bias = small[TAPS + 5 : TAPS + 5 + units // 128].reshape(units)
-    return (block_out, grad_state, grads[0], grads[1], grad_kernel, grad_vectors, grad_up_bias)
+    grad_state = state_grad_call(slot, here, grad_window, grad, cotangent, mask, kernel)
+
+    grad_up, grad_down, grad_kernel, grad_vectors, grad_up_bias = total_call(pieces, units)
+    grad_up_bias = grad_up_bias.reshape(units)
+    return (block_out, grad_state, grad_up, grad_down, grad_kernel, grad_vectors, grad_up_bias)
 
 
 def solution(mesh):

time: 139 us -> 123 us (0.88)
  starting transfers between devices: 32 us -> 21 us
  other arithmetic: 4.91 us -> 1.23 us
  waiting for transfers between devices: 0.02 us -> 3.21 us
  Pallas kernels: 94.9 us -> 92 us
  local copies, waits for them, and re-layouts: 5.73 us -> 3.9 us
    ppermute x8 -> x4, starting transfers between devices: 20.1 us -> 13.5 us  [shifted(): return lax.ppermute(shard, axis, pairs)]
    all_to_all x1, starting transfers between devices: 11.9 us -> 6.3 us  [per_device(): pieces = lax.all_to_all(pieces, 'tx', 0, 0, tiled=True)]
    pallas_call x1, Pallas kernels: 32.2 us -> 28.7 us  [mlp_call(): pl.pallas_call(mlp_kernel, grid_spec=grid_spec, out_shape=[jax.ShapeDtype...]
    ppermute x0 -> x4, waiting for transfers between devices: none -> 3.19 us  [the longest x2 1.84 us: relayed(): return lax.ppermute(jnp.where(odd, below, above), 'tx', pair_pairs())]
    convert_element_type x3 -> x0, other arithmetic: 2.7 us -> none  [the longest x1 0.97 us: per_device(): gup.astype(BF16).reshape(count, -1, chans)]
    slice x3 -> x0, local copies, waits for them, and re-layouts: 1.82 us -> none  [the longest x1 0.61 us: per_device(): grads = (totals[:share], totals[share:2 * share])]
    pallas_call x1 -> x2, Pallas kernels: 18.5 us -> 20.1 us  [the longest x1 18.2 us: own_conv_call(): pl.pallas_call(own_conv_kernel, grid=(slots, edge // STEP_ROWS), in_specs...]
  transfers between devices with their start and end apart: 9 -> 9, of which waited for: 0 -> 3; matrix products, arithmetic and copies ran while one was open for 4% -> 1% of each run, Pallas kernels for 43% -> 48%
where the time goes in v1:
time: 123 us; the launch traced here: 122 us
  Pallas kernels  92 us (75%)
  starting transfers between devices  21 us (17%)
  local copies, waits for them, and re-layouts  3.9 us (3%)
  waiting for transfers between devices  3.21 us (3%)
  other arithmetic  1.23 us (1%)
    pallas_call x1, Pallas kernels, mlp_call(): pl.pallas_call(mlp_kernel, grid_spec=grid_spec, out_shape=[jax.ShapeDtype...  28.7 us
    pallas_call x1, Pallas kernels, tap_grad_call(): pl.pallas_call(tap_grad_kernel, grid_spec=grid_spec, out_shape=jax.ShapeD...  20.8 us
    pallas_call x1, Pallas kernels, state_grad_call(): pl.pallas_call(state_grad_kernel, grid_spec=grid_spec, out_shape=jax.Shap...  19.8 us
    pallas_call x1, Pallas kernels, own_conv_call(): pl.pallas_call(own_conv_kernel, grid=(slots, edge // STEP_ROWS), in_specs...  18.2 us
    ppermute x4, starting transfers between devices, shifted(): return lax.ppermute(shard, axis, pairs)  13.5 us
    all_to_all x1, starting transfers between devices, per_device(): pieces = lax.all_to_all(pieces, 'tx', 0, 0, tiled=True)  6.3 us
    pallas_call x1, Pallas kernels, bands_call(): pl.pallas_call(bands_kernel, grid=(slots,), in_specs=[pl.BlockSpec((1, ed...  2.54 us
  transfers between devices with their start and end apart: 9, of which 3 were waited for; matrix products, arithmetic and copies ran while one was open for 1% of the time, Pallas kernels for 48%

profile of v1, /device:TPU:0, one launch (start us, length us, event | category | flops | bytes accessed | tf_op | source)
XLA Modules:
  0.0 122.2 jit_solution(2853338953777609582)
XLA Ops:
  0.6 1.5 %reshape.20.mask_ref.refs_8_.refs_6_.refs_7_ = s32[2,64,64]{2,1,0:T(8,128)} reshape(s32[2,4096]{1,0:T(2,128)} %param.16) | data formatting | bytes 65536 | tf_op jit(solution)/shard_map/reshape | solution.py:775
  2.1 2.5 %bands.1.refs_2_ = bf16[2,4,3,64,128]{4,3,2,1,0:T(8,128)(2,1)} custom-call(bf16[2,64,64,128]{3,2,1,0:T(8,128)(2,1)} %refs_5_.1, s32[2,64,64]{2,1,0:T(8,128)} %reshape.20.mask_ref.refs_8_.refs_6_.refs_7_), custom_call_target="tpu_custom_call" | custom-call | tf_op jit(solution)/shard_map/bands/pallas_call | solution.py:73
  4.7 1.3 %collective-permute-start.1 = (bf16[2,4,3,64,128]{4,3,2,1,0:T(8,128)(2,1)}, bf16[2,4,3,64,128]{4,3,2,1,0:T(8,128)(2,1)S(1)}, u32[]{:S(2)}, u32[]{:S(2)}) collective-permute-start(bf16[2,4,3,64,128]{4,3,2,1,0:T(8,128)(2,1)} %bands.1.refs_2_), channel_id=1, source_target_pairs={{2,0},{3,1},{4,2},{5,3},{6,4},{7,5},{8,6},{9,7},{10,8},{11,9},{12,... | collective-permute-start | bytes 1179656 | tf_op jit(solution)/shard_map/ppermute | solution.py:34
  6.0 5.5 %collective-permute-start = (bf16[2,4,3,64,128]{4,3,2,1,0:T(8,128)(2,1)}, bf16[2,4,3,64,128]{4,3,2,1,0:T(8,128)(2,1)S(1)}, u32[]{:S(2)}, u32[]{:S(2)}) collective-permute-start(bf16[2,4,3,64,128]{4,3,2,1,0:T(8,128)(2,1)} %bands.1.refs_2_), channel_id=1, source_target_pairs={{0,2},{1,3},{2,4},{3,5},{4,6},{5,7},{6,8},{7,9},{8,10},{9,11},{10,... | collective-permute-start | bytes 1179656 | tf_op jit(solution)/shard_map/ppermute | solution.py:34
  11.5 0.1 collective-permute-start.3
  11.5 0.0 copy-start.10
  11.6 18.2 %own_conv.1.refs_5_ = f32[2,64,64,128]{3,2,1,0:T(8,128)} custom-call(bf16[2,64,64,128]{3,2,1,0:T(8,128)(2,1)} %refs_5_.1, s32[2,64,64]{2,1,0:T(8,128)} %reshape.20.mask_ref.refs_8_.refs_6_.refs_7_, f32[49,128]{1,0:T(8,128)} %refs_8_.1), custom_call_target="tpu_custom_call" | custom-call | flops 102760448 | bytes 8388608 | tf_op jit(solution)/shard_map/own_conv/pallas_call | solution.py:171
  29.8 0.0 collective-permute-done.1.refs_4_
  29.8 0.0 copy-start.1
  29.8 0.0 collective-permute-done.refs_0_
  29.8 0.0 copy-start.2
  29.9 0.5 collective-permute-start.2
  30.4 0.0 copy-done.10
  30.4 0.6 compare_convert_fusion.here_ref
  31.0 0.6 and_select_fusion.slot_ref
  31.6 0.0 collective-permute-done.3.refs_3_
  31.6 0.0 copy-start.5
  31.6 0.2 collective-permute-done.2.refs_1_
  31.8 0.0 copy-start.7
  31.8 0.0 copy-done.1
  31.8 0.0 copy-done.2
  31.8 0.6 copy-done.5
  32.3 0.2 copy-done.7
  32.5 28.7 %mlp.1 = (bf16[2,64,64,128]{3,2,1,0:T(8,128)(2,1)}, f32[2,64,64,128]{3,2,1,0:T(8,128)}, bf16[2,4,3,64,128]{4,3,2,1,0:T(8,128)(2,1)}, f32[512,128]{1,0:T(8,128)},...) custom-call(s32[2,8]{1,0:T(2,128)} %and_select_fusion.slot_ref, ...), custom_call_target="tpu_custom_call" | custom-call | flops 6442450944 | bytes 14680064 | tf_op jit(solution)/shard_map/mlp/pallas_call | solution.py:513
  61.2 1.3 %collective-permute-start.5 = (bf16[2,4,3,64,128]{4,3,2,1,0:T(8,128)(2,1)}, bf16[2,4,3,64,128]{4,3,2,1,0:T(8,128)(2,1)S(1)}, u32[]{:S(2)}, u32[]{:S(2)}) collective-permute-start(bf16[2,4,3,64,128]{4,3,2,1,0:T(8,128)(2,1)} %get-tuple-element.32.refs_2_), channel_id=1, source_target_pairs={{2,0},{3,1},{4,2},{5,3},{6,4},{7,5},{8,6},{9,7},{10,8},{11,9},{12,... | collective-permute-start | bytes 1179656 | tf_op jit(solution)/shard_map/ppermute | solution.py:34
  62.5 5.5 %collective-permute-start.4 = (bf16[2,4,3,64,128]{4,3,2,1,0:T(8,128)(2,1)}, bf16[2,4,3,64,128]{4,3,2,1,0:T(8,128)(2,1)S(1)}, u32[]{:S(2)}, u32[]{:S(2)}) collective-permute-start(bf16[2,4,3,64,128]{4,3,2,1,0:T(8,128)(2,1)} %get-tuple-element.32.refs_2_), channel_id=1, source_target_pairs={{0,2},{1,3},{2,4},{3,5},{4,6},{5,7},{6,8},{7,9},{8,10},{9,11},{10,... | collective-permute-start | bytes 1179656 | tf_op jit(solution)/shard_map/ppermute | solution.py:34
  68.0 20.8 %tap_grad.1 = bf16[16,192,128]{2,1,0:T(8,128)(2,1)} custom-call(s32[2,8]{1,0:T(2,128)} %and_select_fusion.slot_ref, s32[2,8]{1,0:T(2,128)} %compare_convert_fusion.here_ref, bf16[2,4,3,64,128]{4,3,2,1,0:T(8,128)(2,1)} %copy-done.2, bf16[2,4,3,64,128]{4,3,2,1,0:T(8,128)(2,1)} %copy-done.7, bf16[2,4,3,64,128]{4,3,2,1,0:T(8,128)(2,1)} %bands.1.refs_2_, ...), custom_call_target="tpu_custom_call" | custom-call | flops 102760448 | bytes 8388608 | tf_op jit(solution)/shard_map/tap_grad/pallas_call | solution.py:623
  88.8 0.0 copy-start.6
  88.8 0.0 collective-permute-done.5.refs_4_
  88.8 0.0 copy-start.3
  88.8 0.0 collective-permute-done.4.refs_0_
  88.8 0.0 copy-start.4
  88.9 0.1 collective-permute-start.6
  89.0 1.6 %collective-permute-done.6.refs_1_ = bf16[2,4,3,64,128]{4,3,2,1,0:T(8,128)(2,1)S(1)} collective-permute-done((bf16[2,4,3,64,128]{4,3,2,1,0:T(8,128)(2,1)S(1)}, bf16[2,4,3,64,128]{4,3,2,1,0:T(8,128)(2,1)S(1)}, u32[]{:S(2)}, u32[]{:S(2)}) %collective-permute-start.6) | collective-permute-done | bytes 393248 | tf_op jit(solution)/shard_map/ppermute | solution.py:746
  90.7 0.0 copy-start.8
  90.7 6.3 %all-to-all-start = ((bf16[16,192,128]{2,1,0:T(8,128)(2,1)}), bf16[16,192,128]{2,1,0:T(8,128)(2,1)S(1)}, u32[]{:S(2)}, u32[]{:S(2)}) async-start(bf16[16,192,128]{2,1,0:T(8,128)(2,1)} %tap_grad.1), calls=%async_computation | async-start | bytes 1572864 | tf_op jit(solution)/shard_map/all_to_all | solution.py:805
  97.0 0.0 copy-done.6
  97.0 0.5 collective-permute-start.7
  97.5 1.3 %collective-permute-done.7.refs_3_ = bf16[2,4,3,64,128]{4,3,2,1,0:T(8,128)(2,1)S(1)} collective-permute-done((bf16[2,4,3,64,128]{4,3,2,1,0:T(8,128)(2,1)S(1)}, bf16[2,4,3,64,128]{4,3,2,1,0:T(8,128)(2,1)S(1)}, u32[]{:S(2)}, u32[]{:S(2)}) %collective-permute-start.7) | collective-permute-done | bytes 393248 | tf_op jit(solution)/shard_map/ppermute | solution.py:739
  98.8 0.0 copy-done.3
  98.8 0.0 copy-done.4
  98.8 0.0 copy-done.8
  98.8 0.0 copy-start.9
  98.8 0.8 copy-done.9
  99.6 19.8 %state_grad.1 = bf16[2,64,64,128]{3,2,1,0:T(8,128)(2,1)} custom-call(s32[2,8]{1,0:T(2,128)} %and_select_fusion.slot_ref, s32[2,8]{1,0:T(2,128)} %compare_convert_fusion.here_ref, bf16[2,4,3,64,128]{4,3,2,1,0:T(8,128)(2,1)} %copy-done.4, bf16[2,4,3,64,128]{4,3,2,1,0:T(8,128)(2,1)} %copy-done.8, bf16[2,4,3,64,128]{4,3,2,1,0:T(8,128)(2,1)} %get-tuple-element.32.refs_2_, ...), custom_call_target="tpu_custom_call" | custom-call | flops 102760448 | bytes 8388608 | tf_op jit(solution)/shard_map/state_grad/pallas_call | solution.py:696
  119.4 0.0 all-to-all-done.pieces_ref
  119.5 0.0 copy-start
  119.5 0.9 copy-done
  120.4 1.8 %total.1 = (f32[32,128]{1,0:T(8,128)}, f32[32,128]{1,0:T(8,128)}, f32[49,128]{1,0:T(8,128)}, f32[5,128]{1,0:T(8,128)}, f32[4,128]{1,0:T(4,128)}) custom-call(bf16[16,192,128]{2,1,0:T(8,128)(2,1)} %copy-done), custom_call_target="tpu_custom_call" | custom-call | tf_op jit(solution)/shard_map/total/pallas_call | solution.py:724
  (2 shorter events, 0.1 us)
Async XLA Ops:
  4.7 25.1 %collective-permute-start.1 = (bf16[2,4,3,64,128]{4,3,2,1,0:T(8,128)(2,1)}, bf16[2,4,3,64,128]{4,3,2,1,0:T(8,128)(2,1)S(1)}, u32[]{:S(2)}, u32[]{:S(2)}) collective-permute-start(bf16[2,4,3,64,128]{4,3,2,1,0:T(8,128)(2,1)} %bands.1.refs_2_), channel_id=1, source_target_pairs={{2,0},{3,1},{4,2},{5,3},{6,4},{7,5},{8,6},{9,7},{10,8},{11,9},{12,... | collective-permute-start | bytes 1179656 | tf_op jit(solution)/shard_map/ppermute | solution.py:34
  6.0 23.9 %collective-permute-start = (bf16[2,4,3,64,128]{4,3,2,1,0:T(8,128)(2,1)}, bf16[2,4,3,64,128]{4,3,2,1,0:T(8,128)(2,1)S(1)}, u32[]{:S(2)}, u32[]{:S(2)}) collective-permute-start(bf16[2,4,3,64,128]{4,3,2,1,0:T(8,128)(2,1)} %bands.1.refs_2_), channel_id=1, source_target_pairs={{0,2},{1,3},{2,4},{3,5},{4,6},{5,7},{6,8},{7,9},{8,10},{9,11},{10,... | collective-permute-start | bytes 1179656 | tf_op jit(solution)/shard_map/ppermute | solution.py:34
  11.5 20.1 %collective-permute-start.3 = (bf16[2,4,3,64,128]{4,3,2,1,0:T(8,128)(2,1)}, bf16[2,4,3,64,128]{4,3,2,1,0:T(8,128)(2,1)S(1)}, u32[]{:S(2)}, u32[]{:S(2)}) collective-permute-start(bf16[2,4,3,64,128]{4,3,2,1,0:T(8,128)(2,1)} %bands.1.refs_2_), channel_id=1, source_target_pairs={{0,1},{1,0},{2,3},{3,2},{4,5},{5,4},{6,7},{7,6},{8,9},{9,8},{10,11... | collective-permute-start | bytes 1179656 | tf_op jit(solution)/shard_map/ppermute | solution.py:739
  11.5 18.9 %copy-start.10 = (s32[2,8]{1,0:T(2,128)S(1)}, s32[2,8]{1,0:T(2,128)}, u32[]{:S(2)}) copy-start(s32[2,8]{1,0:T(2,128)} %param.15) | copy-start | bytes 196
  29.8 2.0 %copy-start.1 = (bf16[2,4,3,64,128]{4,3,2,1,0:T(8,128)(2,1)}, bf16[2,4,3,64,128]{4,3,2,1,0:T(8,128)(2,1)S(1)}, u32[]{:S(2)}) copy-start(bf16[2,4,3,64,128]{4,3,2,1,0:T(8,128)(2,1)S(1)} %collective-permute-done.1.refs_4_) | copy-start | bytes 1179652
  29.8 1.9 %copy-start.2 = (bf16[2,4,3,64,128]{4,3,2,1,0:T(8,128)(2,1)}, bf16[2,4,3,64,128]{4,3,2,1,0:T(8,128)(2,1)S(1)}, u32[]{:S(2)}) copy-start(bf16[2,4,3,64,128]{4,3,2,1,0:T(8,128)(2,1)S(1)} %collective-permute-done.refs_0_) | copy-start | bytes 1179652
  29.9 1.9 %collective-permute-start.2 = (bf16[2,4,3,64,128]{4,3,2,1,0:T(8,128)(2,1)S(1)}, bf16[2,4,3,64,128]{4,3,2,1,0:T(8,128)(2,1)S(1)}, u32[]{:S(2)}, u32[]{:S(2)}) collective-permute-start(bf16[2,4,3,64,128]{4,3,2,1,0:T(8,128)(2,1)S(1)} %broadcast_select_fusion.1), channel_id=1, source_target_pairs={{0,1},{1,0},{2,3},{3,2},{4,5},{5,4},{6,7},{7,6},{8,9},{9,8},{10,11... | collective-permute-start | bytes 1179656 | tf_op jit(solution)/shard_map/ppermute | solution.py:746
  31.6 0.8 copy-start.5
  31.8 0.7 copy-start.7
  61.2 27.6 %collective-permute-start.5 = (bf16[2,4,3,64,128]{4,3,2,1,0:T(8,128)(2,1)}, bf16[2,4,3,64,128]{4,3,2,1,0:T(8,128)(2,1)S(1)}, u32[]{:S(2)}, u32[]{:S(2)}) collective-permute-start(bf16[2,4,3,64,128]{4,3,2,1,0:T(8,128)(2,1)} %get-tuple-element.32.refs_2_), channel_id=1, source_target_pairs={{2,0},{3,1},{4,2},{5,3},{6,4},{7,5},{8,6},{9,7},{10,8},{11,9},{12,... | collective-permute-start | bytes 1179656 | tf_op jit(solution)/shard_map/ppermute | solution.py:34
  62.5 26.3 %collective-permute-start.4 = (bf16[2,4,3,64,128]{4,3,2,1,0:T(8,128)(2,1)}, bf16[2,4,3,64,128]{4,3,2,1,0:T(8,128)(2,1)S(1)}, u32[]{:S(2)}, u32[]{:S(2)}) collective-permute-start(bf16[2,4,3,64,128]{4,3,2,1,0:T(8,128)(2,1)} %get-tuple-element.32.refs_2_), channel_id=1, source_target_pairs={{0,2},{1,3},{2,4},{3,5},{4,6},{5,7},{6,8},{7,9},{8,10},{9,11},{10,... | collective-permute-start | bytes 1179656 | tf_op jit(solution)/shard_map/ppermute | solution.py:34
  88.8 8.2 %copy-start.6 = (bf16[2,4,3,64,128]{4,3,2,1,0:T(8,128)(2,1)S(1)}, bf16[2,4,3,64,128]{4,3,2,1,0:T(8,128)(2,1)}, u32[]{:S(2)}) copy-start(bf16[2,4,3,64,128]{4,3,2,1,0:T(8,128)(2,1)} %get-tuple-element.32.refs_2_) | copy-start | bytes 1179652
  88.8 10.0 %copy-start.3 = (bf16[2,4,3,64,128]{4,3,2,1,0:T(8,128)(2,1)}, bf16[2,4,3,64,128]{4,3,2,1,0:T(8,128)(2,1)S(1)}, u32[]{:S(2)}) copy-start(bf16[2,4,3,64,128]{4,3,2,1,0:T(8,128)(2,1)S(1)} %collective-permute-done.5.refs_4_) | copy-start | bytes 1179652
  88.8 10.0 %copy-start.4 = (bf16[2,4,3,64,128]{4,3,2,1,0:T(8,128)(2,1)}, bf16[2,4,3,64,128]{4,3,2,1,0:T(8,128)(2,1)S(1)}, u32[]{:S(2)}) copy-start(bf16[2,4,3,64,128]{4,3,2,1,0:T(8,128)(2,1)S(1)} %collective-permute-done.4.refs_0_) | copy-start | bytes 1179652
  88.9 1.8 %collective-permute-start.6 = (bf16[2,4,3,64,128]{4,3,2,1,0:T(8,128)(2,1)S(1)}, bf16[2,4,3,64,128]{4,3,2,1,0:T(8,128)(2,1)S(1)}, u32[]{:S(2)}, u32[]{:S(2)}) collective-permute-start(bf16[2,4,3,64,128]{4,3,2,1,0:T(8,128)(2,1)S(1)} %broadcast_select_fusion), channel_id=1, source_target_pairs={{0,1},{1,0},{2,3},{3,2},{4,5},{5,4},{6,7},{7,6},{8,9},{9,8},{10,11... | collective-permute-start | bytes 1179656 | tf_op jit(solution)/shard_map/ppermute | solution.py:746
  90.7 8.2 %copy-start.8 = (bf16[2,4,3,64,128]{4,3,2,1,0:T(8,128)(2,1)}, bf16[2,4,3,64,128]{4,3,2,1,0:T(8,128)(2,1)S(1)}, u32[]{:S(2)}) copy-start(bf16[2,4,3,64,128]{4,3,2,1,0:T(8,128)(2,1)S(1)} %collective-permute-done.6.refs_1_) | copy-start | bytes 1179652
  90.7 28.8 %all-to-all-start = ((bf16[16,192,128]{2,1,0:T(8,128)(2,1)}), bf16[16,192,128]{2,1,0:T(8,128)(2,1)S(1)}, u32[]{:S(2)}, u32[]{:S(2)}) async-start(bf16[16,192,128]{2,1,0:T(8,128)(2,1)} %tap_grad.1), calls=%async_computation | async-start | bytes 1572864 | tf_op jit(solution)/shard_map/all_to_all | solution.py:805
  97.0 1.8 %collective-permute-start.7 = (bf16[2,4,3,64,128]{4,3,2,1,0:T(8,128)(2,1)S(1)}, bf16[2,4,3,64,128]{4,3,2,1,0:T(8,128)(2,1)S(1)}, u32[]{:S(2)}, u32[]{:S(2)}) collective-permute-start(bf16[2,4,3,64,128]{4,3,2,1,0:T(8,128)(2,1)S(1)} %copy-done.6), channel_id=1, source_target_pairs={{0,1},{1,0},{2,3},{3,2},{4,5},{5,4},{6,7},{7,6},{8,9},{9,8},{10,11... | collective-permute-start | bytes 1179656 | tf_op jit(solution)/shard_map/ppermute | solution.py:739
  98.8 0.8 copy-start.9
  119.5 0.9 copy-start

commit v2 on v1

--- a/solution.py
+++ b/solution.py
@@ -16,6 +16,7 @@
 FCHUNK = 256
 CELLS = 256
 STEP_ROWS = 16
+TAP_ROWS = 32
 VMEM_MIB = 58
 
 EPSILON = 1e-06
@@ -47,17 +48,17 @@
     return [wide[:, r * chans : (r + 1) * chans] for r in range(height)]
 
 
-def bands_kernel(state_ref, mask_ref, out_ref, left, right):
-    edge = state_ref.shape[1]
+def bands_kernel(top_ref, low_ref, left_ref, right_ref, mask_ref, out_ref, left, right):
+    edge = mask_ref.shape[1]
     low = edge - HALO
     upper = mask_ref[0, 0:8].astype(F32).T
     lower = mask_ref[0, edge - 8 :].astype(F32).T
     for q in range(HALO):
-        out_ref[0, 0, q] = (state_ref[0, q].astype(F32) * upper[:, q : q + 1]).astype(BF16)
+        out_ref[0, 0, q] = (top_ref[0, q].astype(F32) * upper[:, q : q + 1]).astype(BF16)
         p = 8 - HALO + q
-        out_ref[0, 1, q] = (state_ref[0, low + q].astype(F32) * lower[:, p : p + 1]).astype(BF16)
-    left[...] = state_ref[0, :, 0:16].astype(F32).reshape(left.shape)
-    right[...] = state_ref[0, :, edge - 16 :].astype(F32).reshape(right.shape)
+        out_ref[0, 1, q] = (low_ref[0, p].astype(F32) * lower[:, p : p + 1]).astype(BF16)
+    left[...] = left_ref[0].astype(F32).reshape(left.shape)
+    right[...] = right_ref[0].astype(F32).reshape(right.shape)
     for q in range(HALO):
         out_ref[0, 2, q] = (
             left[pl.ds(q, edge, stride=16), :] * mask_ref[0, :, q : q + 1].astype(F32)
@@ -74,7 +75,10 @@
         bands_kernel,
         grid=(slots,),
         in_specs=[
-            pl.BlockSpec((1, edge, edge, chans), lambda s: (s, 0, 0, 0)),
+            pl.BlockSpec((1, 8, edge, chans), lambda s: (s, 0, 0, 0)),
+            pl.BlockSpec((1, 8, edge, chans), lambda s: (s, edge // 8 - 1, 0, 0)),
+            pl.BlockSpec((1, edge, 16, chans), lambda s: (s, 0, 0, 0)),
+            pl.BlockSpec((1, edge, 16, chans), lambda s: (s, 0, edge // 16 - 1, 0)),
             pl.BlockSpec((1, edge, edge), lambda s: (s, 0, 0)),
         ],
         out_specs=pl.BlockSpec((1, 4, HALO, edge, chans), lambda s: (s, 0, 0, 0, 0)),
@@ -82,7 +86,7 @@
         scratch_shapes=[pltpu.VMEM((edge * 16, chans), F32)] * 2,
         compiler_params=params(VMEM_MIB),
         name="bands",
-    )(state, mask)
+    )(state, state, state, state, mask)
 
 
 def tap(weight_ref, index, chans):
@@ -203,12 +207,19 @@
         copy.wait()
 
 
-def picked(window, slot_ref, here_ref, tile, direction, which, q):
-    band = window[slot_ref[tile, direction], which, q].astype(F32)
-    return jnp.where(here_ref[tile, direction] > 0, band, jnp.zeros_like(band))
-
-
-def fill_rows(north, south, window, slot_ref, here_ref, tile):
+def picked(window, table_ref, me_ref, tile, direction, which, q):
+    slots = window.shape[0] // (2 * REACH + 1)
+    me, entry = me_ref[0], table_ref[tile, direction]
+    slot = jnp.clip(entry - (me - REACH) * slots, 0, (2 * REACH + 1) * slots - 1)
+    place = lax.div(slot, slots)
+    odd = lax.rem(me, 2) == 1
+    shift = jnp.where(place == 1, 2 * slots, jnp.where(place == 3, -2 * slots, 0))
+    slot = slot + jnp.where(odd, shift, 0)
+    band = window[slot, which, q].astype(F32)
+    return jnp.where(entry >= 0, band, jnp.zeros_like(band))
+
+
+def fill_rows(north, south, window, table_ref, me_ref, tile):
     edge = window.shape[3]
     low = edge - HALO
     for q in range(HALO):
@@ -217,36 +228,36 @@
             (south, 1, 0, 6, 7),
         ):
             target[q, HALO : HALO + edge] = picked(
-                window, slot_ref, here_ref, tile, edge_dir, which, q
+                window, table_ref, me_ref, tile, edge_dir, which, q
             )
-            target[q, 0:HALO] = picked(window, slot_ref, here_ref, tile, left_dir, which, q)[low:]
+            target[q, 0:HALO] = picked(window, table_ref, me_ref, tile, left_dir, which, q)[low:]
             target[q, HALO + edge : HALO + edge + HALO] = picked(
-                window, slot_ref, here_ref, tile, right_dir, which, q
+                window, table_ref, me_ref, tile, right_dir, which, q
             )[0:HALO]
 
 
-def fill_columns(west, east, window, slot_ref, here_ref, tile):
+def fill_columns(west, east, window, table_ref, me_ref, tile):
     edge = window.shape[3]
     for q in range(HALO):
         west[pl.ds(HALO * 16 + q, edge, stride=16), :] = picked(
-            window, slot_ref, here_ref, tile, 2, 3, q
+            window, table_ref, me_ref, tile, 2, 3, q
         )
         east[pl.ds(HALO * 16 + 8 + HALO + q, edge, stride=16), :] = picked(
-            window, slot_ref, here_ref, tile, 3, 2, q
+            window, table_ref, me_ref, tile, 3, 2, q
         )
 
 
-def fill_margins(padded, window, slot_ref, here_ref, tile):
+def fill_margins(padded, window, table_ref, me_ref, tile):
     rows, stride, chans = padded.shape
     edge = window.shape[3]
-    fill_rows(padded.at[0:HALO], padded.at[HALO + edge :], window, slot_ref, here_ref, tile)
+    fill_rows(padded.at[0:HALO], padded.at[HALO + edge :], window, table_ref, me_ref, tile)
     flat = padded.reshape(rows * stride, chans)
     for q in range(HALO):
         flat[pl.ds(HALO * stride + q, edge, stride=stride), :] = picked(
-            window, slot_ref, here_ref, tile, 2, 3, q
+            window, table_ref, me_ref, tile, 2, 3, q
         )
         flat[pl.ds(HALO * stride + HALO + edge + q, edge, stride=stride), :] = picked(
-            window, slot_ref, here_ref, tile, 3, 2, q
+            window, table_ref, me_ref, tile, 3, 2, q
         )
 
 
@@ -308,7 +319,7 @@
     ]
 
 
-def margin_setup(sources, slot_ref, here_ref, scratch):
+def margin_setup(sources, table_ref, me_ref, scratch):
     window, sem, north, south, west, east = scratch
     tile, block = pl.program_id(0), pl.program_id(1)
 
@@ -319,8 +330,8 @@
 
     @pl.when(block == 0)
     def _():
-        fill_rows(north, south, window, slot_ref, here_ref, tile)
-        fill_columns(west, east, window, slot_ref, here_ref, tile)
+        fill_rows(north, south, window, table_ref, me_ref, tile)
+        fill_columns(west, east, window, table_ref, me_ref, tile)
 
 
 def margin_add(weight_ref, target, scratch, chans):
@@ -407,7 +418,7 @@
     return results
 
 
-def mlp_kernel(slot_ref, here_ref, *refs):
+def mlp_kernel(table_ref, me_ref, *refs):
     sources = refs[:5]
     conv_ref, state_ref, cot_ref, mask_ref, weight_ref = refs[5:10]
     bias, gain, nbias, wup, upb, wdown, dbias, scale = refs[10:18]
@@ -428,7 +439,7 @@
         wdown_t[...] = wdown[...].astype(F32).T.astype(BF16)
         upb_s[...] = jnp.broadcast_to(upb[...], (128, upb.shape[1])).T
 
-    margin_setup(sources, slot_ref, here_ref, scratch)
+    margin_setup(sources, table_ref, me_ref, scratch)
     conv_s[...] = conv_ref[0]
     margin_add(weight_ref, conv_s, scratch, chans)
     rows = CELLS // edge
@@ -454,7 +465,7 @@
             state = state_ref[0, place].astype(F32).reshape(CELLS, chans)
             output = (state + (mask * scale[...]) * branch).astype(BF16)
             out_ref[0, place] = output.reshape(rows, edge, chans)
-            grad_ref[0, place] = dconv.reshape(rows, edge, chans)
+            grad_ref[0, place] = dconv.astype(BF16).reshape(rows, edge, chans)
             start = pl.multiple_of((block * height + first) * edge, CELLS)
             tile_grad[pl.ds(start, CELLS), :] = dconv
         return carry
@@ -470,7 +481,7 @@
             bands_ref[0, 3, q] = tile_grad[pl.ds(low + q, edge, stride=edge), :].astype(BF16)
 
 
-def mlp_call(slot, here, sources, conv, state, cot, mask, weights, par):
+def mlp_call(table, me, sources, conv, state, cot, mask, weights, par):
     slots, edge, _, chans = state.shape
     units = par[3].shape[0]
     blocks = edge // STEP_ROWS
@@ -515,7 +526,7 @@
         grid_spec=grid_spec,
         out_shape=[
             jax.ShapeDtypeStruct(state.shape, BF16),
-            jax.ShapeDtypeStruct(state.shape, F32),
+            jax.ShapeDtypeStruct(state.shape, BF16),
             jax.ShapeDtypeStruct((slots, 4, HALO, edge, chans), BF16),
             jax.ShapeDtypeStruct((units, chans), F32),
             jax.ShapeDtypeStruct((units, chans), F32),
@@ -527,52 +538,70 @@
             flops=12 * cells * units * chans, bytes_accessed=14 * cells * chans, transcendentals=0
         ),
         name="mlp",
-    )(slot, here, *sources, conv, state, cot, mask, weights, *par)
-
-
-def tap_grad_kernel(slot_ref, here_ref, *refs):
+    )(table, me, *sources, conv, state, cot, mask, weights, *par)
+
+
+def tap_grad_kernel(table_ref, me_ref, *refs):
     sources = refs[:5]
-    state_ref, mask_ref, grad_ref, gup, gdown, upacc, vec, out_ref = refs[5:13]
-    padded, totals, small = refs[13:16]
-    window, sem = refs[16:]
+    state_ref, mask_ref, grad_ref = refs[5:8]
+    late, out_ref = refs[8:12], refs[12]
+    padded, totals, small, grad_s = refs[13:17]
+    gup, gdown, upacc, vec = refs[17:21]
+    late_sem, window, sem = refs[21:]
     tile, tiles = pl.program_id(0), pl.num_programs(0)
-    edge, chans = grad_ref.shape[1], grad_ref.shape[3]
-
-    @pl.when(tile == 0)
+    block, blocks = pl.program_id(1), pl.num_programs(1)
+    height, edge, chans = grad_s.shape
+
+    def late_copies():
+        return [
+            pltpu.make_async_copy(source, target, late_sem.at[k])
+            for k, (source, target) in enumerate(zip(late, (gup, gdown, upacc, vec)))
+        ]
+
+    @pl.when((tile == 0) & (block == 0))
     def _():
         start_window(sources, window, sem)
+        for copy in late_copies():
+            copy.start()
         totals[...] = jnp.zeros_like(totals)
         zero_margins(padded)
 
-    fill_masked(padded, state_ref, mask_ref)
-
-    @pl.when(tile == 0)
+    @pl.when(block == 0)
+    def _():
+        fill_masked(padded, state_ref, mask_ref)
+
+    @pl.when((tile == 0) & (block == 0))
     def _():
         wait_window(sources, window, sem)
 
-    fill_margins(padded, window, slot_ref, here_ref, tile)
-
+    @pl.when(block == 0)
+    def _():
+        fill_margins(padded, window, table_ref, me_ref, tile)
+
+    grad_s[...] = grad_ref[0].astype(F32)
     for b in range(KSIZE):
 
         def body(n, sums, b=b):
             sums = list(sums)
-            row = n * ROWS
             for g in range(edge // 8):
-                grads = [grad_ref[0, row + i, g * 8 : g * 8 + 8] for i in range(ROWS)]
-                for r in range(ROWS + KSIZE - 1):
-                    cells = padded[row + r, pl.ds(g * 8 + b, 8), :]
+                grads = [grad_s[n * CONV_ROWS + i, g * 8 : g * 8 + 8] for i in range(CONV_ROWS)]
+                for r in range(CONV_ROWS + KSIZE - 1):
+                    row = block * height + n * CONV_ROWS + r
+                    cells = padded[row, pl.ds(g * 8 + b, 8), :]
                     for a in range(KSIZE):
-                        if 0 <= r - a < ROWS:
+                        if 0 <= r - a < CONV_ROWS:
                             sums[a] = sums[a] + cells * grads[r - a]
             return tuple(sums)
 
         start = tuple(totals[a * KSIZE + b] for a in range(KSIZE))
-        sums = lax.fori_loop(0, edge // ROWS, body, start)
+        sums = lax.fori_loop(0, height // CONV_ROWS, body, start)
         for a in range(KSIZE):
             totals[a * KSIZE + b] = sums[a]
 
-    @pl.when(tile == tiles - 1)
-    def _():
+    @pl.when((tile == tiles - 1) & (block == blocks - 1))
+    def _():
+        for copy in late_copies():
+            copy.wait()
         small[...] = jnp.zeros_like(small)
         small[0:TAPS] = jnp.sum(totals[...], 1)
         small[TAPS : TAPS + 5] = jnp.sum(vec[...], 1)
@@ -593,30 +622,32 @@
             out_ref[d, 2 * share + rows :] = rest
 
 
-def tap_grad_call(slot, here, sources, state, mask, grad, gup, gdown, upacc, vec, count):
+def tap_grad_call(table, me, sources, state, mask, grad, gup, gdown, upacc, vec, count):
     slots, edge, _, chans = state.shape
     rows = TAPS + 5 + upacc.shape[0] // 128
     rows = -(-rows // 16) * 16
     length = 2 * (upacc.shape[0] // count) + 2 * rows
-    tile_spec = pl.BlockSpec((1, edge, edge, chans), lambda s, *_: (s, 0, 0, 0))
     grid_spec = pltpu.PrefetchScalarGridSpec(
         num_scalar_prefetch=2,
-        grid=(slots,),
+        grid=(slots, edge // TAP_ROWS),
         in_specs=[pl.BlockSpec(memory_space=pl.ANY)] * 5
         + [
-            tile_spec,
-            pl.BlockSpec((1, edge, edge), lambda s, *_: (s, 0, 0)),
-            tile_spec,
-            pl.BlockSpec(gup.shape, lambda s, *_: (0, 0)),
-            pl.BlockSpec(gdown.shape, lambda s, *_: (0, 0)),
-            pl.BlockSpec(upacc.shape, lambda s, *_: (0, 0)),
-            pl.BlockSpec(vec.shape, lambda s, *_: (0, 0, 0)),
-        ],
-        out_specs=pl.BlockSpec((count, length, chans), lambda s, *_: (0, 0, 0)),
+            pl.BlockSpec((1, edge, edge, chans), lambda s, n, *_: (s, 0, 0, 0)),
+            pl.BlockSpec((1, edge, edge), lambda s, n, *_: (s, 0, 0)),
+            pl.BlockSpec((1, TAP_ROWS, edge, chans), lambda s, n, *_: (s, n, 0, 0)),
+        ]
+        + [pl.BlockSpec(memory_space=pl.ANY)] * 4,
+        out_specs=pl.BlockSpec((count, length, chans), lambda s, n, *_: (0, 0, 0)),
         scratch_shapes=[
             pltpu.VMEM(padded_shape(edge, chans), F32),
             pltpu.VMEM((TAPS, 8, chans), F32),
             pltpu.VMEM((rows, chans), F32),
+            pltpu.VMEM((TAP_ROWS, edge, chans), F32),
+            pltpu.VMEM(gup.shape, F32),
+            pltpu.VMEM(gdown.shape, F32),
+            pltpu.VMEM(upacc.shape, F32),
+            pltpu.VMEM(vec.shape, F32),
+            pltpu.SemaphoreType.DMA((4,)),
         ]
         + window_scratch(slots, edge, chans),
     )
@@ -627,66 +658,65 @@
         compiler_params=params(VMEM_MIB),
         cost_estimate=conv_cost(slots, edge, chans),
         name="tap_grad",
-    )(slot, here, *sources, state, mask, grad, gup, gdown, upacc, vec)
-
-
-def state_grad_kernel(slot_ref, here_ref, *refs):
+    )(table, me, *sources, state, mask, grad, gup, gdown, upacc, vec)
+
+
+def state_grad_kernel(table_ref, me_ref, *refs):
     sources = refs[:5]
     grad_ref, cot_ref, mask_ref, weight_ref, out_ref, padded, conv_s, window, sem = refs[5:]
-    tile = pl.program_id(0)
+    tile, block = pl.program_id(0), pl.program_id(1)
     edge, chans = grad_ref.shape[1], grad_ref.shape[3]
 
-    @pl.when(tile == 0)
+    @pl.when((tile == 0) & (block == 0))
     def _():
         start_window(sources, window, sem)
         zero_margins(padded)
 
-    def fill(n, carry):
+    @pl.when(block == 0)
+    def _():
+        def fill(n, carry):
+            for r in range(8):
+                i = n * 8 + r
+                padded[HALO + i, HALO : HALO + edge] = grad_ref[0, i].astype(F32)
+            return carry
+
+        lax.fori_loop(0, edge // 8, fill, 0)
+
+    @pl.when((tile == 0) & (block == 0))
+    def _():
+        wait_window(sources, window, sem)
+
+    @pl.when(block == 0)
+    def _():
+        fill_margins(padded, window, table_ref, me_ref, tile)
+
+    for g in range(edge // 8):
+
+        def write(i, value):
+            conv_s[i, g * 8 : g * 8 + 8] = value
+
+        conv_rows(padded, weight_ref, block * CONV_ROWS, g * 8, write, chans, True)
+    for k in range(0, CONV_ROWS, 8):
+        slabs = spread(mask_ref[0, k : k + 8], chans)
         for r in range(8):
-            i = n * 8 + r
-            padded[HALO + i, HALO : HALO + edge] = grad_ref[0, i]
-        return carry
-
-    lax.fori_loop(0, edge // 8, fill, 0)
-
-    @pl.when(tile == 0)
-    def _():
-        wait_window(sources, window, sem)
-
-    fill_margins(padded, window, slot_ref, here_ref, tile)
-
-    def body(n, carry):
-        row = n * CONV_ROWS
-        for g in range(edge // 8):
-
-            def write(i, value):
-                conv_s[i, g * 8 : g * 8 + 8] = value
-
-            conv_rows(padded, weight_ref, row, g * 8, write, chans, True)
-        for k in range(0, CONV_ROWS, 8):
-            slabs = spread(mask_ref[0, pl.ds(pl.multiple_of(row + k, 8), 8)], chans)
-            for r in range(8):
-                i = row + k + r
-                out_ref[0, i] = (cot_ref[0, i].astype(F32) + slabs[r] * conv_s[k + r]).astype(BF16)
-        return carry
-
-    lax.fori_loop(0, edge // CONV_ROWS, body, 0)
-
-
-def state_grad_call(slot, here, sources, grad, cot, mask, weights):
+            i = k + r
+            out_ref[0, i] = (cot_ref[0, i].astype(F32) + slabs[r] * conv_s[i]).astype(BF16)
+
+
+def state_grad_call(table, me, sources, grad, cot, mask, weights):
     slots, edge, _, chans = cot.shape
-    tile_spec = pl.BlockSpec((1, edge, edge, chans), lambda s, *_: (s, 0, 0, 0))
+    row_spec = pl.BlockSpec((1, CONV_ROWS, edge, chans), lambda s, n, *_: (s, n, 0, 0))
     grid_spec = pltpu.PrefetchScalarGridSpec(
         num_scalar_prefetch=2,
-        grid=(slots,),
+        grid=(slots, edge // CONV_ROWS),
         in_specs=[pl.BlockSpec(memory_space=pl.ANY)] * 5
         + [
-            tile_spec,
-            tile_spec,
-            pl.BlockSpec((1, edge, edge), lambda s, *_: (s, 0, 0)),
-            pl.BlockSpec((TAPS, chans), lambda s, *_: (0, 0)),
+            pl.BlockSpec((1, edge, edge, chans), lambda s, n, *_: (s, 0, 0, 0)),
+            row_spec,
+            pl.BlockSpec((1, CONV_ROWS, edge), lambda s, n, *_: (s, n, 0)),
+            pl.BlockSpec((TAPS, chans), lambda s, n, *_: (0, 0)),
         ],
-        out_specs=tile_spec,
+        out_specs=row_spec,
         scratch_shapes=[
             pltpu.VMEM(padded_shape(edge, chans), F32),
             pltpu.VMEM((CONV_ROWS, edge, chans), F32),
@@ -700,7 +730,7 @@
         compiler_params=params(VMEM_MIB),
         cost_estimate=conv_cost(slots, edge, chans),
         name="state_grad",
-    )(slot, here, *sources, grad, cot, mask, weights)
+    )(table, me, *sources, grad, cot, mask, weights)
 
 
 def total_kernel(pieces_ref, up_ref, down_ref, taps_ref, vec_ref, bias_ref):
@@ -744,14 +774,6 @@
 def relayed(below, above):
     odd = lax.axis_index("tx") % 2 == 1
     return lax.ppermute(jnp.where(odd, below, above), "tx", pair_pairs())
-
-
-def window_slots(neighbours, slots):
-    me = lax.axis_index("tx")
-    low = (me - REACH) * slots
-    slot = jnp.clip(neighbours - low, 0, (2 * REACH + 1) * slots - 1)
-    swap = (me % 2 == 1) & ((slot // slots == 1) | (slot // slots == 3))
-    return jnp.where(swap, slot + jnp.where(slot // slots == 1, 2, -2) * slots, slot)
 
 
 def per_device(
@@ -773,8 +795,7 @@
     units = w_up.shape[0]
     count = lax.axis_size("tx")
     mask = land_mask.reshape(slots, edge, edge)
-    here = (neighbours >= 0).astype(jnp.int32)
-    slot = window_slots(neighbours, slots)
+    me = lax.axis_index("tx").astype(jnp.int32)[None]
     par = (
         conv_bias[None],
         norm_gain[None],
@@ -788,22 +809,23 @@
 
     bands = bands_call(tile_state, mask)
     below, partner, above = direct(bands)
+    conv = own_conv_call(tile_state, mask, kernel)
+    below, above, conv = lax.optimization_barrier((below, above, conv))
     window = [below, relayed(below, above), bands, partner, above]
-    conv = own_conv_call(tile_state, mask, kernel)
     block_out, grad, grad_bands, gup, gdown, upacc, vec = mlp_call(
-        slot, here, window, conv, tile_state, cotangent, mask, kernel, par
+        neighbours, me, window, conv, tile_state, cotangent, mask, kernel, par
     )
     below, partner, above = direct(grad_bands)
 
     pieces = tap_grad_call(
-        slot, here, window, tile_state, mask, grad, gup, gdown, upacc, vec, count
+        neighbours, me, window, tile_state, mask, grad, gup, gdown, upacc, vec, count
     )
     pieces, below, above, grad = lax.optimization_barrier((pieces, below, above, grad))
     relay = relayed(below, above)
     pieces, relay, grad = lax.optimization_barrier((pieces, relay, grad))
     grad_window = [below, relay, grad_bands, partner, above]
     pieces = lax.all_to_all(pieces, "tx", 0, 0, tiled=True)
-    grad_state = state_grad_call(slot, here, grad_window, grad, cotangent, mask, kernel)
+    grad_state = state_grad_call(neighbours, me, grad_window, grad, cotangent, mask, kernel)
 
     grad_up, grad_down, grad_kernel, grad_vectors, grad_up_bias = total_call(pieces, units)
     grad_up_bias = grad_up_bias.reshape(units)

time: 123 us -> 122 us (level)
  transfers between devices with their start and end apart: 9 -> 9, of which waited for: 3 -> 3; matrix products, arithmetic and copies ran while one was open for 1% -> 0% of each run, Pallas kernels for 48% -> 48%
where the time goes in v2:
time: 122 us; the launch traced here: 121 us
  Pallas kernels  90.8 us (74%)
  starting transfers between devices  21 us (17%)
  waiting for transfers between devices  4.36 us (4%)
  local copies, waits for them, and re-layouts  3.86 us (3%)
    pallas_call x1, Pallas kernels, mlp_call(): pl.pallas_call(mlp_kernel, grid_spec=grid_spec, out_shape=[jax.ShapeDtype...  28.8 us
    pallas_call x1, Pallas kernels, tap_grad_call(): pl.pallas_call(tap_grad_kernel, grid_spec=grid_spec, out_shape=jax.ShapeD...  20.2 us
    pallas_call x1, Pallas kernels, state_grad_call(): pl.pallas_call(state_grad_kernel, grid_spec=grid_spec, out_shape=jax.Shap...  19.2 us
    pallas_call x1, Pallas kernels, own_conv_call(): pl.pallas_call(own_conv_kernel, grid=(slots, edge // STEP_ROWS), in_specs...  18.2 us
    ppermute x4, starting transfers between devices, shifted(): return lax.ppermute(shard, axis, pairs)  13.5 us
    all_to_all x1, starting transfers between devices, per_device(): pieces = lax.all_to_all(pieces, 'tx', 0, 0, tiled=True)  6.3 us
    ppermute x2, waiting for transfers between devices, relayed(): return lax.ppermute(jnp.where(odd, below, above), 'tx', pair_pairs())  2.99 us
    pallas_call x1, Pallas kernels, bands_call(): pl.pallas_call(bands_kernel, grid=(slots,), in_specs=[pl.BlockSpec((1, 8,...  2.49 us
  transfers between devices with their start and end apart: 9, of which 3 were waited for; matrix products, arithmetic and copies ran while one was open for 0% of the time, Pallas kernels for 48%

profile of v2, /device:TPU:0, one launch (start us, length us, event | category | flops | bytes accessed | tf_op | source)
XLA Modules:
  0.0 121.0 jit_solution(1311770063460316934)
XLA Ops:
  0.6 1.5 %reshape.20.mask_ref.refs_8_.refs_6_.refs_7_ = s32[2,64,64]{2,1,0:T(8,128)} reshape(s32[2,4096]{1,0:T(2,128)} %param.16) | data formatting | bytes 65536 | tf_op jit(solution)/shard_map/reshape | solution.py:797
  2.1 2.5 %bands.1.refs_2_ = bf16[2,4,3,64,128]{4,3,2,1,0:T(8,128)(2,1)} custom-call(bf16[2,64,64,128]{3,2,1,0:T(8,128)(2,1)} %refs_5_.1, bf16[2,64,64,128]{3,2,1,0:T(8,128)(2,1)} %refs_5_.1, bf16[2,64,64,128]{3,2,1,0:T(8,128)(2,1)} %refs_5_.1, bf16[2,64,64,128]{3,2,1,0:T(8,128)(2,1)} %refs_5_.1, s32[2,64,64]{2,1,0:T(8,128)} %reshape.20.mask_ref.refs_8_.refs_6_.refs_7_), custom_call_target="tpu_custom_call" | custom-call | tf_op jit(solution)/shard_map/bands/pallas_call | solution.py:74
  4.6 1.3 %collective-permute-start.1 = (bf16[2,4,3,64,128]{4,3,2,1,0:T(8,128)(2,1)}, bf16[2,4,3,64,128]{4,3,2,1,0:T(8,128)(2,1)S(1)}, u32[]{:S(2)}, u32[]{:S(2)}) collective-permute-start(bf16[2,4,3,64,128]{4,3,2,1,0:T(8,128)(2,1)} %bands.1.refs_2_), channel_id=1, source_target_pairs={{2,0},{3,1},{4,2},{5,3},{6,4},{7,5},{8,6},{9,7},{10,8},{11,9},{12,... | collective-permute-start | bytes 1179656 | tf_op jit(solution)/shard_map/ppermute | solution.py:35
  5.9 5.5 %collective-permute-start = (bf16[2,4,3,64,128]{4,3,2,1,0:T(8,128)(2,1)}, bf16[2,4,3,64,128]{4,3,2,1,0:T(8,128)(2,1)S(1)}, u32[]{:S(2)}, u32[]{:S(2)}) collective-permute-start(bf16[2,4,3,64,128]{4,3,2,1,0:T(8,128)(2,1)} %bands.1.refs_2_), channel_id=1, source_target_pairs={{0,2},{1,3},{2,4},{3,5},{4,6},{5,7},{6,8},{7,9},{8,10},{9,11},{10,... | collective-permute-start | bytes 1179656 | tf_op jit(solution)/shard_map/ppermute | solution.py:35
  11.4 0.1 collective-permute-start.3
  11.5 18.2 %own_conv.1.refs_5_ = f32[2,64,64,128]{3,2,1,0:T(8,128)} custom-call(bf16[2,64,64,128]{3,2,1,0:T(8,128)(2,1)} %refs_5_.1, s32[2,64,64]{2,1,0:T(8,128)} %reshape.20.mask_ref.refs_8_.refs_6_.refs_7_, f32[49,128]{1,0:T(8,128)} %refs_8_.1), custom_call_target="tpu_custom_call" | custom-call | flops 102760448 | bytes 8388608 | tf_op jit(solution)/shard_map/own_conv/pallas_call | solution.py:175
  29.7 0.0 collective-permute-done.1.refs_4_
  29.7 0.0 copy-start.3
  29.7 0.0 collective-permute-done.refs_0_
  29.7 0.0 copy-start.4
  29.8 0.5 collective-permute-start.2
  30.3 0.0 collective-permute-done.3.refs_3_
  30.3 0.0 copy-start.8
  30.3 1.3 %collective-permute-done.2.refs_1_ = bf16[2,4,3,64,128]{4,3,2,1,0:T(8,128)(2,1)S(1)} collective-permute-done((bf16[2,4,3,64,128]{4,3,2,1,0:T(8,128)(2,1)S(1)}, bf16[2,4,3,64,128]{4,3,2,1,0:T(8,128)(2,1)S(1)}, u32[]{:S(2)}, u32[]{:S(2)}) %collective-permute-start.2) | collective-permute-done | bytes 393248 | tf_op jit(solution)/shard_map/ppermute | solution.py:776
  31.6 0.0 copy-start.9
  31.6 0.0 copy-done.3
  31.6 0.0 copy-done.4
  31.6 0.0 copy-done.8
  31.6 0.7 copy-done.9
  32.4 28.8 %mlp.1 = (bf16[2,64,64,128]{3,2,1,0:T(8,128)(2,1)}, bf16[2,64,64,128]{3,2,1,0:T(8,128)(2,1)}, bf16[2,4,3,64,128]{4,3,2,1,0:T(8,128)(2,1)}, f32[512,128]{1,0:T(8,...) custom-call(s32[2,8]{1,0:T(2,128)} %table_ref.5, s32[1]{0:T(128)} %bitcast.me_ref, ...), custom_call_target="tpu_custom_call" | custom-call | flops 6442450944 | bytes 14680064 | tf_op jit(solution)/shard_map/mlp/pallas_call | solution.py:524
  61.2 1.3 %collective-permute-start.5 = (bf16[2,4,3,64,128]{4,3,2,1,0:T(8,128)(2,1)}, bf16[2,4,3,64,128]{4,3,2,1,0:T(8,128)(2,1)S(1)}, u32[]{:S(2)}, u32[]{:S(2)}) collective-permute-start(bf16[2,4,3,64,128]{4,3,2,1,0:T(8,128)(2,1)} %get-tuple-element.38.refs_2_), channel_id=1, source_target_pairs={{2,0},{3,1},{4,2},{5,3},{6,4},{7,5},{8,6},{9,7},{10,8},{11,9},{12,... | collective-permute-start | bytes 1179656 | tf_op jit(solution)/shard_map/ppermute | solution.py:35
  62.5 5.5 %collective-permute-start.4 = (bf16[2,4,3,64,128]{4,3,2,1,0:T(8,128)(2,1)}, bf16[2,4,3,64,128]{4,3,2,1,0:T(8,128)(2,1)S(1)}, u32[]{:S(2)}, u32[]{:S(2)}) collective-permute-start(bf16[2,4,3,64,128]{4,3,2,1,0:T(8,128)(2,1)} %get-tuple-element.38.refs_2_), channel_id=1, source_target_pairs={{0,2},{1,3},{2,4},{3,5},{4,6},{5,7},{6,8},{7,9},{8,10},{9,11},{10,... | collective-permute-start | bytes 1179656 | tf_op jit(solution)/shard_map/ppermute | solution.py:35
  68.0 20.2 %tap_grad.1 = bf16[16,192,128]{2,1,0:T(8,128)(2,1)} custom-call(s32[2,8]{1,0:T(2,128)} %table_ref.5, s32[1]{0:T(128)} %bitcast.me_ref, bf16[2,4,3,64,128]{4,3,2,1,0:T(8,128)(2,1)} %copy-done.4, bf16[2,4,3,64,128]{4,3,2,1,0:T(8,128)(2,1)} %copy-done.9, bf16[2,4,3,64,128]{4,3,2,1,0:T(8,128)(2,1)} %bands.1.refs_2_, bf16[2,4,3,64,128]{4,3,2,1,0:T(8,128)(2,1)} %copy-done.8, ...), custom_call_target="tpu_custom_call" | custom-call | flops 102760448 | bytes 8388608 | tf_op jit(solution)/shard_map/tap_grad/pallas_call | solution.py:654
  88.2 0.0 copy-start.5
  88.2 0.0 collective-permute-done.5.refs_4_
  88.2 0.0 copy-start.1
  88.2 0.0 collective-permute-done.4.refs_0_
  88.2 0.0 copy-start.2
  88.3 0.1 collective-permute-start.6
  88.4 1.6 %collective-permute-done.6.refs_1_ = bf16[2,4,3,64,128]{4,3,2,1,0:T(8,128)(2,1)S(1)} collective-permute-done((bf16[2,4,3,64,128]{4,3,2,1,0:T(8,128)(2,1)S(1)}, bf16[2,4,3,64,128]{4,3,2,1,0:T(8,128)(2,1)S(1)}, u32[]{:S(2)}, u32[]{:S(2)}) %collective-permute-start.6) | collective-permute-done | bytes 393248 | tf_op jit(solution)/shard_map/ppermute | solution.py:776
  90.1 0.0 copy-start.6
  90.1 6.3 %all-to-all-start = ((bf16[16,192,128]{2,1,0:T(8,128)(2,1)}), bf16[16,192,128]{2,1,0:T(8,128)(2,1)S(1)}, u32[]{:S(2)}, u32[]{:S(2)}) async-start(bf16[16,192,128]{2,1,0:T(8,128)(2,1)} %tap_grad.1), calls=%async_computation | async-start | bytes 1572864 | tf_op jit(solution)/shard_map/all_to_all | solution.py:827
  96.4 0.0 copy-done.5
  96.4 0.5 collective-permute-start.7
  96.9 1.3 %collective-permute-done.7.refs_3_ = bf16[2,4,3,64,128]{4,3,2,1,0:T(8,128)(2,1)S(1)} collective-permute-done((bf16[2,4,3,64,128]{4,3,2,1,0:T(8,128)(2,1)S(1)}, bf16[2,4,3,64,128]{4,3,2,1,0:T(8,128)(2,1)S(1)}, u32[]{:S(2)}, u32[]{:S(2)}) %collective-permute-start.7) | collective-permute-done | bytes 393248 | tf_op jit(solution)/shard_map/ppermute | solution.py:769
  98.2 0.0 copy-done.1
  98.2 0.0 copy-done.2
  98.2 0.0 copy-done.6
  98.2 0.0 copy-start.7
  98.2 0.8 copy-done.7
  99.0 19.2 %state_grad.1 = bf16[2,64,64,128]{3,2,1,0:T(8,128)(2,1)} custom-call(s32[2,8]{1,0:T(2,128)} %table_ref.5, s32[1]{0:T(128)} %bitcast.me_ref, bf16[2,4,3,64,128]{4,3,2,1,0:T(8,128)(2,1)} %copy-done.2, bf16[2,4,3,64,128]{4,3,2,1,0:T(8,128)(2,1)} %copy-done.6, bf16[2,4,3,64,128]{4,3,2,1,0:T(8,128)(2,1)} %get-tuple-element.38.refs_2_, ...), custom_call_target="tpu_custom_call" | custom-call | flops 102760448 | bytes 8388608 | tf_op jit(solution)/shard_map/state_grad/pallas_call | solution.py:726
  118.3 0.0 all-to-all-done.pieces_ref
  118.3 0.0 copy-start
  118.3 0.9 copy-done
  119.1 1.8 %total.1 = (f32[32,128]{1,0:T(8,128)}, f32[32,128]{1,0:T(8,128)}, f32[49,128]{1,0:T(8,128)}, f32[5,128]{1,0:T(8,128)}, f32[4,128]{1,0:T(4,128)}) custom-call(bf16[16,192,128]{2,1,0:T(8,128)(2,1)} %copy-done), custom_call_target="tpu_custom_call" | custom-call | tf_op jit(solution)/shard_map/total/pallas_call | solution.py:754
  (2 shorter events, 0.1 us)
Async XLA Ops:
  4.6 25.1 %collective-permute-start.1 = (bf16[2,4,3,64,128]{4,3,2,1,0:T(8,128)(2,1)}, bf16[2,4,3,64,128]{4,3,2,1,0:T(8,128)(2,1)S(1)}, u32[]{:S(2)}, u32[]{:S(2)}) collective-permute-start(bf16[2,4,3,64,128]{4,3,2,1,0:T(8,128)(2,1)} %bands.1.refs_2_), channel_id=1, source_target_pairs={{2,0},{3,1},{4,2},{5,3},{6,4},{7,5},{8,6},{9,7},{10,8},{11,9},{12,... | collective-permute-start | bytes 1179656 | tf_op jit(solution)/shard_map/ppermute | solution.py:35
  5.9 23.8 %collective-permute-start = (bf16[2,4,3,64,128]{4,3,2,1,0:T(8,128)(2,1)}, bf16[2,4,3,64,128]{4,3,2,1,0:T(8,128)(2,1)S(1)}, u32[]{:S(2)}, u32[]{:S(2)}) collective-permute-start(bf16[2,4,3,64,128]{4,3,2,1,0:T(8,128)(2,1)} %bands.1.refs_2_), channel_id=1, source_target_pairs={{0,2},{1,3},{2,4},{3,5},{4,6},{5,7},{6,8},{7,9},{8,10},{9,11},{10,... | collective-permute-start | bytes 1179656 | tf_op jit(solution)/shard_map/ppermute | solution.py:35
  11.4 18.9 %collective-permute-start.3 = (bf16[2,4,3,64,128]{4,3,2,1,0:T(8,128)(2,1)}, bf16[2,4,3,64,128]{4,3,2,1,0:T(8,128)(2,1)S(1)}, u32[]{:S(2)}, u32[]{:S(2)}) collective-permute-start(bf16[2,4,3,64,128]{4,3,2,1,0:T(8,128)(2,1)} %bands.1.refs_2_), channel_id=1, source_target_pairs={{0,1},{1,0},{2,3},{3,2},{4,5},{5,4},{6,7},{7,6},{8,9},{9,8},{10,11... | collective-permute-start | bytes 1179656 | tf_op jit(solution)/shard_map/ppermute | solution.py:769
  29.7 2.0 %copy-start.3 = (bf16[2,4,3,64,128]{4,3,2,1,0:T(8,128)(2,1)}, bf16[2,4,3,64,128]{4,3,2,1,0:T(8,128)(2,1)S(1)}, u32[]{:S(2)}) copy-start(bf16[2,4,3,64,128]{4,3,2,1,0:T(8,128)(2,1)S(1)} %collective-permute-done.1.refs_4_) | copy-start | bytes 1179652
  29.7 1.9 %copy-start.4 = (bf16[2,4,3,64,128]{4,3,2,1,0:T(8,128)(2,1)}, bf16[2,4,3,64,128]{4,3,2,1,0:T(8,128)(2,1)S(1)}, u32[]{:S(2)}) copy-start(bf16[2,4,3,64,128]{4,3,2,1,0:T(8,128)(2,1)S(1)} %collective-permute-done.refs_0_) | copy-start | bytes 1179652
  29.8 1.9 %collective-permute-start.2 = (bf16[2,4,3,64,128]{4,3,2,1,0:T(8,128)(2,1)S(1)}, bf16[2,4,3,64,128]{4,3,2,1,0:T(8,128)(2,1)S(1)}, u32[]{:S(2)}, u32[]{:S(2)}) collective-permute-start(bf16[2,4,3,64,128]{4,3,2,1,0:T(8,128)(2,1)S(1)} %broadcast_select_fusion.1), channel_id=1, source_target_pairs={{0,1},{1,0},{2,3},{3,2},{4,5},{5,4},{6,7},{7,6},{8,9},{9,8},{10,11... | collective-permute-start | bytes 1179656 | tf_op jit(solution)/shard_map/ppermute | solution.py:776
  30.3 1.4 %copy-start.8 = (bf16[2,4,3,64,128]{4,3,2,1,0:T(8,128)(2,1)}, bf16[2,4,3,64,128]{4,3,2,1,0:T(8,128)(2,1)S(1)}, u32[]{:S(2)}) copy-start(bf16[2,4,3,64,128]{4,3,2,1,0:T(8,128)(2,1)S(1)} %collective-permute-done.3.refs_3_) | copy-start | bytes 1179652
  31.6 0.7 copy-start.9
  61.2 27.0 %collective-permute-start.5 = (bf16[2,4,3,64,128]{4,3,2,1,0:T(8,128)(2,1)}, bf16[2,4,3,64,128]{4,3,2,1,0:T(8,128)(2,1)S(1)}, u32[]{:S(2)}, u32[]{:S(2)}) collective-permute-start(bf16[2,4,3,64,128]{4,3,2,1,0:T(8,128)(2,1)} %get-tuple-element.38.refs_2_), channel_id=1, source_target_pairs={{2,0},{3,1},{4,2},{5,3},{6,4},{7,5},{8,6},{9,7},{10,8},{11,9},{12,... | collective-permute-start | bytes 1179656 | tf_op jit(solution)/shard_map/ppermute | solution.py:35
  62.5 25.7 %collective-permute-start.4 = (bf16[2,4,3,64,128]{4,3,2,1,0:T(8,128)(2,1)}, bf16[2,4,3,64,128]{4,3,2,1,0:T(8,128)(2,1)S(1)}, u32[]{:S(2)}, u32[]{:S(2)}) collective-permute-start(bf16[2,4,3,64,128]{4,3,2,1,0:T(8,128)(2,1)} %get-tuple-element.38.refs_2_), channel_id=1, source_target_pairs={{0,2},{1,3},{2,4},{3,5},{4,6},{5,7},{6,8},{7,9},{8,10},{9,11},{10,... | collective-permute-start | bytes 1179656 | tf_op jit(solution)/shard_map/ppermute | solution.py:35
  88.2 8.2 %copy-start.5 = (bf16[2,4,3,64,128]{4,3,2,1,0:T(8,128)(2,1)S(1)}, bf16[2,4,3,64,128]{4,3,2,1,0:T(8,128)(2,1)}, u32[]{:S(2)}) copy-start(bf16[2,4,3,64,128]{4,3,2,1,0:T(8,128)(2,1)} %get-tuple-element.38.refs_2_) | copy-start | bytes 1179652
  88.2 10.0 %copy-start.1 = (bf16[2,4,3,64,128]{4,3,2,1,0:T(8,128)(2,1)}, bf16[2,4,3,64,128]{4,3,2,1,0:T(8,128)(2,1)S(1)}, u32[]{:S(2)}) copy-start(bf16[2,4,3,64,128]{4,3,2,1,0:T(8,128)(2,1)S(1)} %collective-permute-done.5.refs_4_) | copy-start | bytes 1179652
  88.2 10.0 %copy-start.2 = (bf16[2,4,3,64,128]{4,3,2,1,0:T(8,128)(2,1)}, bf16[2,4,3,64,128]{4,3,2,1,0:T(8,128)(2,1)S(1)}, u32[]{:S(2)}) copy-start(bf16[2,4,3,64,128]{4,3,2,1,0:T(8,128)(2,1)S(1)} %collective-permute-done.4.refs_0_) | copy-start | bytes 1179652
  88.3 1.8 %collective-permute-start.6 = (bf16[2,4,3,64,128]{4,3,2,1,0:T(8,128)(2,1)S(1)}, bf16[2,4,3,64,128]{4,3,2,1,0:T(8,128)(2,1)S(1)}, u32[]{:S(2)}, u32[]{:S(2)}) collective-permute-start(bf16[2,4,3,64,128]{4,3,2,1,0:T(8,128)(2,1)S(1)} %broadcast_select_fusion), channel_id=1, source_target_pairs={{0,1},{1,0},{2,3},{3,2},{4,5},{5,4},{6,7},{7,6},{8,9},{9,8},{10,11... | collective-permute-start | bytes 1179656 | tf_op jit(solution)/shard_map/ppermute | solution.py:776
  90.1 8.2 %copy-start.6 = (bf16[2,4,3,64,128]{4,3,2,1,0:T(8,128)(2,1)}, bf16[2,4,3,64,128]{4,3,2,1,0:T(8,128)(2,1)S(1)}, u32[]{:S(2)}) copy-start(bf16[2,4,3,64,128]{4,3,2,1,0:T(8,128)(2,1)S(1)} %collective-permute-done.6.refs_1_) | copy-start | bytes 1179652
  90.1 28.2 %all-to-all-start = ((bf16[16,192,128]{2,1,0:T(8,128)(2,1)}), bf16[16,192,128]{2,1,0:T(8,128)(2,1)S(1)}, u32[]{:S(2)}, u32[]{:S(2)}) async-start(bf16[16,192,128]{2,1,0:T(8,128)(2,1)} %tap_grad.1), calls=%async_computation | async-start | bytes 1572864 | tf_op jit(solution)/shard_map/all_to_all | solution.py:827
  96.4 1.8 %collective-permute-start.7 = (bf16[2,4,3,64,128]{4,3,2,1,0:T(8,128)(2,1)S(1)}, bf16[2,4,3,64,128]{4,3,2,1,0:T(8,128)(2,1)S(1)}, u32[]{:S(2)}, u32[]{:S(2)}) collective-permute-start(bf16[2,4,3,64,128]{4,3,2,1,0:T(8,128)(2,1)S(1)} %copy-done.5), channel_id=1, source_target_pairs={{0,1},{1,0},{2,3},{3,2},{4,5},{5,4},{6,7},{7,6},{8,9},{9,8},{10,11... | collective-permute-start | bytes 1179656 | tf_op jit(solution)/shard_map/ppermute | solution.py:769
  98.2 0.8 copy-start.7
  118.3 0.9 copy-start
